TPU v7x, 512 devices: a whole 4x4x16 slice. The times are simulated.
512 devices in a mesh: tile: 64 (over x, z_lo, core), tm: 8 (over z_hi, y).
Axes of the slice: x: 4, y: 4, z: 16 (z_hi: 2, z_lo: 8; z = z_hi * 8 + z_lo), core: 2. Of those that a mesh axis runs over, the one named last changes fastest.
Arguments:
- controls: float32 [16, 512, 8, 512], P('tm', 'tile'), may hold values from -6 to 6
- perturbations: bfloat16 [8, 16, 4, 512, 8, 512], P('tm', None, None, 'tile'), may hold values from -6 to 6
- owner: int32 [16], replicated, may hold values from 0 to 15, each once
- land_mask: int32 [512, 512], P('tile'), may hold values 0 or 1
- diffusivity: float32 [2, 8], replicated, may hold values from 0.2 to 0.24
Outputs:
- increment: float32 [8, 4, 512, 8, 512], P('tm', None, 'tile')
Inputs may be any that keep to these rules, and one draw needn't show every extreme that they name: owner names every member exactly once.
All inputs are finite; a program needn't handle non-finite values. No bound on the sum of `land_mask` on one device may be relied on, other than what follows from the above.
Results may differ from a plain program's by a relative error of at most 0.0029.
Values may be sent and summed in bfloat16 or wider, within the bound.
A program may use at most 64 MiB of HBM per device.

v0:
```python
import math

import jax
import jax.numpy as jnp
from jax import lax
from jax.sharding import PartitionSpec as P

SWEEPS = 4


def with_halo(cells, sides, width):
    for axis, dim in sides:
        count = lax.axis_size(axis)
        ends = count - 1
        head = lax.slice_in_dim(cells, 0, width, axis=dim)
        tail = lax.slice_in_dim(cells, cells.shape[dim] - width, cells.shape[dim], axis=dim)
        cells = jnp.concatenate(
            [
                lax.ppermute(tail, axis, [(i, (i + 1) % count) for i in range(ends)]),
                cells,
                lax.ppermute(head, axis, [((i + 1) % count, i) for i in range(ends)]),
            ],
            axis=dim,
        )
    return cells


def spread(value, axis, source):
    kept = jnp.where(lax.axis_index(axis) == source, value, 0).astype(value.dtype)
    return lax.psum(kept, axis)


def weight_sweep(field, coef):
    padded = jnp.pad(field, ((0, 0), (1, 1), (0, 0), (1, 1)))
    coef_pad = jnp.pad(coef, ((1, 1), (0, 0), (1, 1)))
    flux = 0.5 * (coef + coef_pad[:-2, :, 1:-1]) * (padded[:, :-2, :, 1:-1] - field)
    flux = flux + 0.5 * (coef + coef_pad[2:, :, 1:-1]) * (padded[:, 2:, :, 1:-1] - field)
    flux = flux + 0.5 * (coef + coef_pad[1:-1, :, :-2]) * (padded[:, 1:-1, :, :-2] - field)
    flux = flux + 0.5 * (coef + coef_pad[1:-1, :, 2:]) * (padded[:, 1:-1, :, 2:] - field)
    return field + flux


def on_device(controls, perturbations, owner, land_mask, diffusivity):
    diffuse_coef = jnp.where(
        land_mask[:, None, :] == 1, diffusivity[1][None, :, None], diffusivity[0][None, :, None]
    )
    rim_rows = 1
    coef_wide = with_halo(diffuse_coef, (("tile", 0),), rim_rows)
    smooth = controls
    for sweep_index in range(SWEEPS):
        extended = with_halo(smooth, (("tile", 1),), 1)
        smooth = weight_sweep(extended, coef_wide)[:, 1:-1]
    weights = smooth.astype(jnp.bfloat16)
    member_count = owner.shape[0]
    pert_here = perturbations[0]
    factor = 1.0 / math.sqrt(member_count - 1)
    pair_count = controls.shape[0]
    summed = jnp.zeros(pert_here.shape[1:], jnp.float32)
    for root_index in range(lax.axis_size("tm")):
        arrived = spread(weights, "tm", root_index)
        chosen = lax.dynamic_slice_in_dim(owner, root_index * pair_count, pair_count)
        selected = jnp.take(pert_here, chosen, axis=0)
        summed = summed + jnp.einsum(
            "pvxly,pxly->vxly", selected, arrived, preferred_element_type=jnp.float32
        )
    return (summed * factor)[None]


def solution(mesh):
    return jax.shard_map(
        on_device,
        mesh=mesh,
        in_specs=(
            P("tm", "tile", None, None),
            P("tm", None, None, "tile", None, None),
            P(),
            P("tile", None),
            P(),
        ),
        out_specs=P("tm", None, "tile", None, None),
        check_vma=False,
    )
```

profile of v0, /device:TPU:24, one launch (start us, length us, event | category | flops | bytes accessed | tf_op | source)
XLA Modules:
  0.0 285.7 jit_solution(9800533867567195115)
XLA Ops:
  8.1 1.7 collective-permute-start.2
  9.9 1.3 collective-permute-start.3
  11.9 4.7 %collective-permute-start = (f32[2,1,8,512]{3,2,1,0:T(8,128)S(1)}, f32[2,1,8,512]{3,2,1,0:T(8,128)S(1)}, u32[]{:S(2)}, u32[]{:S(2)}) collective-permute-start(f32[2,1,8,512]{3,2,1,0:T(8,128)S(1)} %get-tuple-element.43), channel_id=1, source_target_pairs={{0,8},{8,16},{16,24},{24,32},{32,40},{40,48},{48,56},{56,64},{64,7... | collective-permute-start | bytes 98312 | tf_op jit(solution)/shard_map/ppermute | solution.py:19
  16.7 1.3 collective-permute-start.1
  19.2 1.8 collective-permute-done.1
  21.3 4.5 %collective-permute-start.4 = (f32[2,1,8,512]{3,2,1,0:T(8,128)S(1)}, f32[2,1,8,512]{3,2,1,0:T(8,128)S(1)}, u32[]{:S(2)}, u32[]{:S(2)}) collective-permute-start(f32[2,1,8,512]{3,2,1,0:T(8,128)S(1)} %get-tuple-element.40), channel_id=1, source_target_pairs={{0,8},{8,16},{16,24},{24,32},{32,40},{40,48},{48,56},{56,64},{64,7... | collective-permute-start | bytes 98312 | tf_op jit(solution)/shard_map/ppermute | solution.py:19
  25.8 1.3 collective-permute-start.5
  27.2 1.8 collective-permute-done.5
  29.3 4.3 %collective-permute-start.6 = (f32[2,1,8,512]{3,2,1,0:T(8,128)S(1)}, f32[2,1,8,512]{3,2,1,0:T(8,128)S(1)}, u32[]{:S(2)}, u32[]{:S(2)}) collective-permute-start(f32[2,1,8,512]{3,2,1,0:T(8,128)S(1)} %get-tuple-element.38), channel_id=1, source_target_pairs={{0,8},{8,16},{16,24},{24,32},{32,40},{40,48},{48,56},{56,64},{64,7... | collective-permute-start | bytes 98312 | tf_op jit(solution)/shard_map/ppermute | solution.py:19
  33.6 1.3 collective-permute-start.7
  34.9 1.8 collective-permute-done.7
  37.0 4.3 %collective-permute-start.8 = (f32[2,1,8,512]{3,2,1,0:T(8,128)S(1)}, f32[2,1,8,512]{3,2,1,0:T(8,128)S(1)}, u32[]{:S(2)}, u32[]{:S(2)}) collective-permute-start(f32[2,1,8,512]{3,2,1,0:T(8,128)S(1)} %get-tuple-element.36), channel_id=1, source_target_pairs={{0,8},{8,16},{16,24},{24,32},{32,40},{40,48},{48,56},{56,64},{64,7... | collective-permute-start | bytes 98312 | tf_op jit(solution)/shard_map/ppermute | solution.py:19
  41.4 1.3 collective-permute-start.9
  42.8 1.7 collective-permute-done.9
  46.7 2.8 gather_fusion.1
  49.5 2.8 gather_fusion
  52.3 2.8 gather_fusion.2
  55.1 2.8 gather_fusion.3
  57.9 3.6 %gather_fusion.4 = bf16[2,4,8,8,512]{4,3,2,1,0:T(8,128)(2,1)} fusion(bf16[16,4,8,8,512]{4,3,2,1,0:T(8,128)(2,1)} %bitcast.45, s32[1024]{0:T(1024)S(1)} %get-tuple-element.84), kind=kCustom, calls=%fused_computation.4.clone | custom fusion | bytes 1048584 | tf_op jit(solution)/shard_map/jit(_take)/gather | solution.py:62
  61.4 2.8 gather_fusion.5
  64.2 3.6 %gather_fusion.6 = bf16[2,4,8,8,512]{4,3,2,1,0:T(8,128)(2,1)} fusion(bf16[16,4,8,8,512]{4,3,2,1,0:T(8,128)(2,1)} %bitcast.47, s32[1024]{0:T(1024)S(1)} %get-tuple-element.82), kind=kCustom, calls=%fused_computation.6.clone | custom fusion | bytes 1048584 | tf_op jit(solution)/shard_map/jit(_take)/gather | solution.py:62
  67.8 2.8 gather_fusion.7
  70.6 200.8 %all-reduce.8.cloned.1.call-done = (bf16[2,8,8,512]{3,2,1,0:T(8,128)(2,1)}, bf16[2,8,8,512]{3,2,1,0:T(8,128)(2,1)}, bf16[2,8,8,512]{3,2,1,0:T(8,128)(2,1)}, bf16...) async-done(((bf16[2,8,8,512]{3,2,1,0:T(8,128)(2,1)}, ...) | async-done | bytes 1048592 | tf_op jit(solution)/shard_map/psum | solution.py:30
  277.5 1.3 multiply_bitcast_fusion
  (60 shorter events, 12.8 us)
Async XLA Ops:
  6.5 264.8 %all-reduce.8.cloned.1.call-start = ((), (), s32[]{:S(2)}) async-start(), calls=%async_computation | async-start | bytes 2097152 | tf_op jit(solution)/shard_map/psum | solution.py:30
  8.1 9.9 %collective-permute-start.2 = (f32[1,8,512]{2,1,0:T(8,128)S(1)}, f32[1,8,512]{2,1,0:T(8,128)S(1)}, u32[]{:S(2)}, u32[]{:S(2)}) collective-permute-start(f32[1,8,512]{2,1,0:T(8,128)S(1)} %get-tuple-element.55), channel_id=1, source_target_pairs={{0,8},{8,16},{16,24},{24,32},{32,40},{40,48},{48,56},{56,64},{64,7... | collective-permute-start | bytes 49160 | tf_op jit(solution)/shard_map/ppermute | solution.py:19
  9.9 8.1 %collective-permute-start.3 = (f32[1,8,512]{2,1,0:T(8,128)S(1)}, f32[1,8,512]{2,1,0:T(8,128)S(1)}, u32[]{:S(2)}, u32[]{:S(2)}) collective-permute-start(f32[1,8,512]{2,1,0:T(8,128)S(1)} %get-tuple-element.56), channel_id=1, source_target_pairs={{8,0},{16,8},{24,16},{32,24},{40,32},{48,40},{56,48},{64,56},{72,6... | collective-permute-start | bytes 49160 | tf_op jit(solution)/shard_map/ppermute | solution.py:21
  11.9 6.2 %collective-permute-start = (f32[2,1,8,512]{3,2,1,0:T(8,128)S(1)}, f32[2,1,8,512]{3,2,1,0:T(8,128)S(1)}, u32[]{:S(2)}, u32[]{:S(2)}) collective-permute-start(f32[2,1,8,512]{3,2,1,0:T(8,128)S(1)} %get-tuple-element.43), channel_id=1, source_target_pairs={{0,8},{8,16},{16,24},{24,32},{32,40},{40,48},{48,56},{56,64},{64,7... | collective-permute-start | bytes 98312 | tf_op jit(solution)/shard_map/ppermute | solution.py:19
  16.7 4.3 %collective-permute-start.1 = (f32[2,1,8,512]{3,2,1,0:T(8,128)S(1)}, f32[2,1,8,512]{3,2,1,0:T(8,128)S(1)}, u32[]{:S(2)}, u32[]{:S(2)}) collective-permute-start(f32[2,1,8,512]{3,2,1,0:T(8,128)S(1)} %get-tuple-element.42), channel_id=1, source_target_pairs={{8,0},{16,8},{24,16},{32,24},{40,32},{48,40},{56,48},{64,56},{72,6... | collective-permute-start | bytes 98312 | tf_op jit(solution)/shard_map/ppermute | solution.py:21
  21.3 5.9 %collective-permute-start.4 = (f32[2,1,8,512]{3,2,1,0:T(8,128)S(1)}, f32[2,1,8,512]{3,2,1,0:T(8,128)S(1)}, u32[]{:S(2)}, u32[]{:S(2)}) collective-permute-start(f32[2,1,8,512]{3,2,1,0:T(8,128)S(1)} %get-tuple-element.40), channel_id=1, source_target_pairs={{0,8},{8,16},{16,24},{24,32},{32,40},{40,48},{48,56},{56,64},{64,7... | collective-permute-start | bytes 98312 | tf_op jit(solution)/shard_map/ppermute | solution.py:19
  25.8 3.1 %collective-permute-start.5 = (f32[2,1,8,512]{3,2,1,0:T(8,128)S(1)}, f32[2,1,8,512]{3,2,1,0:T(8,128)S(1)}, u32[]{:S(2)}, u32[]{:S(2)}) collective-permute-start(f32[2,1,8,512]{3,2,1,0:T(8,128)S(1)} %get-tuple-element.41), channel_id=1, source_target_pairs={{8,0},{16,8},{24,16},{32,24},{40,32},{48,40},{56,48},{64,56},{72,6... | collective-permute-start | bytes 98312 | tf_op jit(solution)/shard_map/ppermute | solution.py:21
  29.3 5.7 %collective-permute-start.6 = (f32[2,1,8,512]{3,2,1,0:T(8,128)S(1)}, f32[2,1,8,512]{3,2,1,0:T(8,128)S(1)}, u32[]{:S(2)}, u32[]{:S(2)}) collective-permute-start(f32[2,1,8,512]{3,2,1,0:T(8,128)S(1)} %get-tuple-element.38), channel_id=1, source_target_pairs={{0,8},{8,16},{16,24},{24,32},{32,40},{40,48},{48,56},{56,64},{64,7... | collective-permute-start | bytes 98312 | tf_op jit(solution)/shard_map/ppermute | solution.py:19
  33.6 3.1 %collective-permute-start.7 = (f32[2,1,8,512]{3,2,1,0:T(8,128)S(1)}, f32[2,1,8,512]{3,2,1,0:T(8,128)S(1)}, u32[]{:S(2)}, u32[]{:S(2)}) collective-permute-start(f32[2,1,8,512]{3,2,1,0:T(8,128)S(1)} %get-tuple-element.39), channel_id=1, source_target_pairs={{8,0},{16,8},{24,16},{32,24},{40,32},{48,40},{56,48},{64,56},{72,6... | collective-permute-start | bytes 98312 | tf_op jit(solution)/shard_map/ppermute | solution.py:21
  37.0 9.6 %copy-start.2 = (s32[16]{0:T(128)S(1)}, s32[16]{0:T(128)}, u32[]{:S(2)}) copy-start(s32[16]{0:T(128)} %param.9) | copy-start | bytes 196
  37.0 5.8 %collective-permute-start.8 = (f32[2,1,8,512]{3,2,1,0:T(8,128)S(1)}, f32[2,1,8,512]{3,2,1,0:T(8,128)S(1)}, u32[]{:S(2)}, u32[]{:S(2)}) collective-permute-start(f32[2,1,8,512]{3,2,1,0:T(8,128)S(1)} %get-tuple-element.36), channel_id=1, source_target_pairs={{0,8},{8,16},{16,24},{24,32},{32,40},{40,48},{48,56},{56,64},{64,7... | collective-permute-start | bytes 98312 | tf_op jit(solution)/shard_map/ppermute | solution.py:19
  41.4 3.1 %collective-permute-start.9 = (f32[2,1,8,512]{3,2,1,0:T(8,128)S(1)}, f32[2,1,8,512]{3,2,1,0:T(8,128)S(1)}, u32[]{:S(2)}, u32[]{:S(2)}) collective-permute-start(f32[2,1,8,512]{3,2,1,0:T(8,128)S(1)} %get-tuple-element.37), channel_id=1, source_target_pairs={{8,0},{16,8},{24,16},{32,24},{40,32},{48,40},{56,48},{64,56},{72,6... | collective-permute-start | bytes 98312 | tf_op jit(solution)/shard_map/ppermute | solution.py:21
  271.3 5.2 %copy-start = (bf16[2,4,8,8,512]{4,3,2,1,0:T(8,128)(2,1)S(1)}, bf16[2,4,8,8,512]{4,3,2,1,0:T(8,128)(2,1)}, u32[]{:S(2)}) copy-start(bf16[2,4,8,8,512]{4,3,2,1,0:T(8,128)(2,1)} %gather_fusion.4) | copy-start | bytes 1572868
  274.5 2.6 copy-start.1
Sparse Core Ops, SparseCore 0:
  46.7 224.5 all-reduce.7
where the time goes:
time: 287 us; the launch traced here: 286 us
  waiting for transfers between devices  208 us (72%)
  local copies, waits for them, and re-layouts  26.4 us (9%)
  starting transfers between devices  26.1 us (9%)
  between operations  13.9 us (5%)
  other arithmetic  11.4 us (4%)
    psum x1, waiting for transfers between devices, spread(): return lax.psum(kept, axis)  201 us
    gather x8, local copies, waits for them, and re-layouts, on_device(): selected = jnp.take(pert_here, chosen, axis=0)  23.7 us
    ppermute x5, starting transfers between devices, with_halo(): lax.ppermute(tail, axis, [(i, (i + 1) % count) for i in range(ends)])  19.7 us
    ppermute x5, waiting for transfers between devices, with_halo(): lax.ppermute(head, axis, [((i + 1) % count, i) for i in range(ends)])  7.04 us
    ppermute x5, starting transfers between devices, with_halo(): lax.ppermute(head, axis, [((i + 1) % count, i) for i in range(ends)])  6.46 us
  transfers between devices with their start and end apart: 11, of which 5 were waited for; matrix products, arithmetic and copies ran while one was open for 9% of the time, Pallas kernels for 0%

commit v1 on v0

v1 whole, which is shorter than its diff:
```python
import math

import jax
import jax.numpy as jnp
from jax import lax
from jax.sharding import PartitionSpec as P

SWEEPS = 4


def halo_rows(cells, width, dim):
    count = lax.axis_size("tile")
    ends = count - 1
    head = lax.slice_in_dim(cells, 0, width, axis=dim)
    tail = lax.slice_in_dim(cells, cells.shape[dim] - width, cells.shape[dim], axis=dim)
    before = lax.ppermute(tail, "tile", [(i, i + 1) for i in range(ends)])
    after = lax.ppermute(head, "tile", [(i + 1, i) for i in range(ends)])
    return jnp.concatenate([before, cells, after], axis=dim)


def weight_sweep(field, coef):
    padded = jnp.pad(field, ((0, 0), (1, 1), (0, 0), (1, 1)))
    coef_pad = jnp.pad(coef, ((1, 1), (0, 0), (1, 1)))
    flux = 0.5 * (coef + coef_pad[:-2, :, 1:-1]) * (padded[:, :-2, :, 1:-1] - field)
    flux = flux + 0.5 * (coef + coef_pad[2:, :, 1:-1]) * (padded[:, 2:, :, 1:-1] - field)
    flux = flux + 0.5 * (coef + coef_pad[1:-1, :, :-2]) * (padded[:, 1:-1, :, :-2] - field)
    flux = flux + 0.5 * (coef + coef_pad[1:-1, :, 2:]) * (padded[:, 1:-1, :, 2:] - field)
    return field + flux


def on_device(controls, perturbations, owner, land_mask, diffusivity):
    rows = controls.shape[1]
    width = SWEEPS
    tile = lax.axis_index("tile")
    count = lax.axis_size("tile")
    grow = tile * rows - width + jnp.arange(rows + 2 * width)
    inside = (grow >= 0) & (grow < count * rows)

    mask_wide = halo_rows(land_mask, width, 0)
    coef = jnp.where(
        mask_wide[:, None, :] == 1, diffusivity[1][None, :, None], diffusivity[0][None, :, None]
    )
    coef = jnp.where(inside[:, None, None], coef, 0.0)
    keep = inside[None, :, None, None]
    smooth = jnp.where(keep, halo_rows(controls, width, 1), 0.0)
    for sweep_index in range(SWEEPS):
        smooth = jnp.where(keep, weight_sweep(smooth, coef), 0.0)
    weights = smooth[:, width:width + rows].astype(jnp.bfloat16)

    every = lax.all_gather(weights, "tm", axis=0, tiled=True)
    by_member = jnp.zeros_like(every).at[owner].set(every)
    member_count = owner.shape[0]
    factor = 1.0 / math.sqrt(member_count - 1)
    summed = jnp.einsum(
        "mvxly,mxly->vxly", perturbations[0], by_member, preferred_element_type=jnp.float32
    )
    return (summed * factor)[None]


def solution(mesh):
    return jax.shard_map(
        on_device,
        mesh=mesh,
        in_specs=(
            P("tm", "tile", None, None),
            P("tm", None, None, "tile", None, None),
            P(),
            P("tile", None),
            P(),
        ),
        out_specs=P("tm", None, "tile", None, None),
        check_vma=False,
    )
```

time: 287 us -> 151 us (0.53)
  the two profiles are of different devices: /device:TPU:24 before, /device:TPU:2 now
where the time goes in v1:
time: 151 us
  waiting for transfers between devices  96 us (64%)
  starting transfers between devices  27.5 us (18%)
  between operations  13.6 us (9%)
  other arithmetic  8.62 us (6%)
  local copies, waits for them, and re-layouts  5.02 us (3%)
    all_gather x1, waiting for transfers between devices, on_device(): every = lax.all_gather(weights, 'tm', axis=0, tiled=True)  95.4 us
    ppermute x2, starting transfers between devices, halo_rows(): after = lax.ppermute(head, 'tile', [(i + 1, i) for i in range(ends)])  23.7 us
    ppermute x2, starting transfers between devices, halo_rows(): before = lax.ppermute(tail, 'tile', [(i, i + 1) for i in range(ends)])  3.83 us
    dot_general x1, other arithmetic, on_device(): jnp.einsum('mvxly,mxly->vxly', perturbations[0], by_member, preferred_ele...  3.17 us
  transfers between devices with their start and end apart: 5, of which 2 were waited for; matrix products, arithmetic and copies ran while one was open for 2% of the time, Pallas kernels for 0%

profile of v1, /device:TPU:2, one launch (start us, length us, event | category | flops | bytes accessed | tf_op | source)
XLA Modules:
  0.0 150.7 jit_solution(17457148186831489938)
XLA Ops:
  6.5 0.8 fusion.59
  7.3 1.9 %collective-permute-start.2 = (s32[4,512]{1,0:T(4,128)S(1)}, s32[4,512]{1,0:T(4,128)S(1)}, u32[]{:S(2)}, u32[]{:S(2)}) collective-permute-start(s32[4,512]{1,0:T(4,128)S(1)} %get-tuple-element.15), channel_id=1, source_target_pairs={{0,8},{8,16},{16,24},{24,32},{32,40},{40,48},{48,56},{56,64},{64,7... | collective-permute-start | bytes 24584 | tf_op jit(solution)/shard_map/ppermute | solution.py:16
  9.3 12.6 %collective-permute-start.3 = (s32[4,512]{1,0:T(4,128)S(1)}, s32[4,512]{1,0:T(4,128)S(1)}, u32[]{:S(2)}, u32[]{:S(2)}) collective-permute-start(s32[4,512]{1,0:T(4,128)S(1)} %get-tuple-element.16), channel_id=1, source_target_pairs={{8,0},{16,8},{24,16},{32,24},{40,32},{48,40},{56,48},{64,56},{72,6... | collective-permute-start | bytes 24584 | tf_op jit(solution)/shard_map/ppermute | solution.py:17
  21.8 1.0 fusion.58
  22.8 1.9 %collective-permute-start = (f32[2,4,8,512]{3,2,1,0:T(8,128)S(1)}, f32[2,4,8,512]{3,2,1,0:T(8,128)S(1)}, u32[]{:S(2)}, u32[]{:S(2)}) collective-permute-start(f32[2,4,8,512]{3,2,1,0:T(8,128)S(1)} %get-tuple-element.13), channel_id=1, source_target_pairs={{0,8},{8,16},{16,24},{24,32},{32,40},{40,48},{48,56},{56,64},{64,7... | collective-permute-start | bytes 393224 | tf_op jit(solution)/shard_map/ppermute | solution.py:16
  24.8 11.1 %collective-permute-start.1 = (f32[2,4,8,512]{3,2,1,0:T(8,128)S(1)}, f32[2,4,8,512]{3,2,1,0:T(8,128)S(1)}, u32[]{:S(2)}, u32[]{:S(2)}) collective-permute-start(f32[2,4,8,512]{3,2,1,0:T(8,128)S(1)} %get-tuple-element.14), channel_id=1, source_target_pairs={{8,0},{16,8},{24,16},{32,24},{40,32},{48,40},{56,48},{64,56},{72,6... | collective-permute-start | bytes 393224 | tf_op jit(solution)/shard_map/ppermute | solution.py:17
  35.9 0.8 slice_bitcast_fusion.1
  36.7 0.1 slice.128
  36.8 0.7 add_compare_fusion
  37.5 0.1 select_select_fusion
  37.6 0.2 fusion.45
  37.9 0.5 collective-permute-done.1
  38.4 1.0 maximum_select_fusion
  39.5 0.4 fusion.6
  39.9 0.4 fusion.19
  40.3 0.4 fusion.32
  40.6 0.3 fusion.40
  41.0 0.8 fusion.56
  41.8 95.4 %all-gather.2.cloned.1.call-done = bf16[16,8,8,512]{3,2,1,0:T(8,128)(2,1)} async-done(((bf16[2,8,8,512]{3,2,1,0:T(8,128)(2,1)}), bf16[16,8,8,512]{3,2,1,0:T(8,128)(2,1)}) %all-gather.2.cloned.1.call-update) | async-done | bytes 1048592 | tf_op jit(solution)/shard_map/all_gather | solution.py:50
  137.2 0.1 broadcast_in_dim.96
  137.3 2.3 %scatter_fusion = bf16[16,8,8,512]{3,2,1,0:T(8,128)(2,1)S(1)} fusion(bf16[16,8,8,512]{3,2,1,0:T(8,128)(2,1)S(1)} %broadcast_in_dim.96, s32[16]{0:T(128)S(1)} %compare_select_fusion, bf16[16,8,8,512]{3,2,1,0:T(8,128)(2,1)} %all-gather.2.cloned.1.call-done), kind=kCustom, calls=%fused_computation | custom fusion | bytes 3145792 | tf_op jit(solution)/shard_map/scatter | solution.py:51
  139.6 0.3 bitcast_convert_fusion
  139.8 3.2 %multiply_reduce_fusion = f32[8,8,512,4]{2,1,0,3:T(8,128)S(1)} fusion(f32[8,8,512,16]{2,1,0,3:T(8,128)S(1)} %bitcast_convert_fusion, bf16[1,16,4,8,8,512]{5,4,3,2,1,0:T(8,128)(2,1)} %param.6), kind=kLoop, calls=%fused_computation.1 | loop fusion | flops 6160384 | bytes 6815744 | tf_op jit(solution)/shard_map/mvxly,mxly->vxly/dot_general | solution.py:54
  143.0 0.8 multiply_bitcast_fusion
  (11 shorter events, 0.1 us)
Async XLA Ops:
  6.5 130.7 %all-gather.2.cloned.1.call-start = ((), (), s32[]{:S(2)}) async-start(), calls=%async_computation | async-start | bytes 1179648 | tf_op jit(solution)/shard_map/all_gather | solution.py:50
  7.3 29.4 %collective-permute-start.2 = (s32[4,512]{1,0:T(4,128)S(1)}, s32[4,512]{1,0:T(4,128)S(1)}, u32[]{:S(2)}, u32[]{:S(2)}) collective-permute-start(s32[4,512]{1,0:T(4,128)S(1)} %get-tuple-element.15), channel_id=1, source_target_pairs={{0,8},{8,16},{16,24},{24,32},{32,40},{40,48},{48,56},{56,64},{64,7... | collective-permute-start | bytes 24584 | tf_op jit(solution)/shard_map/ppermute | solution.py:16
  9.3 27.5 %collective-permute-start.3 = (s32[4,512]{1,0:T(4,128)S(1)}, s32[4,512]{1,0:T(4,128)S(1)}, u32[]{:S(2)}, u32[]{:S(2)}) collective-permute-start(s32[4,512]{1,0:T(4,128)S(1)} %get-tuple-element.16), channel_id=1, source_target_pairs={{8,0},{16,8},{24,16},{32,24},{40,32},{48,40},{56,48},{64,56},{72,6... | collective-permute-start | bytes 24584 | tf_op jit(solution)/shard_map/ppermute | solution.py:17
  22.8 15.0 %collective-permute-start = (f32[2,4,8,512]{3,2,1,0:T(8,128)S(1)}, f32[2,4,8,512]{3,2,1,0:T(8,128)S(1)}, u32[]{:S(2)}, u32[]{:S(2)}) collective-permute-start(f32[2,4,8,512]{3,2,1,0:T(8,128)S(1)} %get-tuple-element.13), channel_id=1, source_target_pairs={{0,8},{8,16},{16,24},{24,32},{32,40},{40,48},{48,56},{56,64},{64,7... | collective-permute-start | bytes 393224 | tf_op jit(solution)/shard_map/ppermute | solution.py:16
  24.8 13.7 %collective-permute-start.1 = (f32[2,4,8,512]{3,2,1,0:T(8,128)S(1)}, f32[2,4,8,512]{3,2,1,0:T(8,128)S(1)}, u32[]{:S(2)}, u32[]{:S(2)}) collective-permute-start(f32[2,4,8,512]{3,2,1,0:T(8,128)S(1)} %get-tuple-element.14), channel_id=1, source_target_pairs={{8,0},{16,8},{24,16},{32,24},{40,32},{48,40},{56,48},{64,56},{72,6... | collective-permute-start | bytes 393224 | tf_op jit(solution)/shard_map/ppermute | solution.py:17
  39.9 1.9 %copy-start = (s32[16]{0:T(128)S(1)}, s32[16]{0:T(128)}, u32[]{:S(2)}) copy-start(s32[16]{0:T(128)} %param.7) | copy-start | bytes 196
Sparse Core Ops, SparseCore 0:
  41.9 95.2 all-gather.1

commit v2 on v1

--- a/solution.py
+++ b/solution.py
@@ -1,9 +1,14 @@
+import functools
 import math
 
 import jax
 import jax.numpy as jnp
 from jax import lax
+from jax.experimental import pallas as pl
+from jax.experimental.pallas import tpu as pltpu
 from jax.sharding import PartitionSpec as P
+
+MESH = pl.DeviceIdType.MESH
 
 SWEEPS = 4
 
@@ -28,6 +33,65 @@
     return field + flux
 
 
+def gather_kernel(half, w_ref, out_ref, send_sem, recv_sem):
+    tile = lax.axis_index("tile")
+    me = lax.axis_index("tm")
+    groups = lax.axis_size("tm")
+    depth = w_ref.shape[0]
+    zp = lax.rem(me + half, groups)
+    base = me - lax.rem(me, half)
+    peers = [base + lax.rem(lax.rem(me, half) + d, half) for d in range(1, half)]
+
+    barrier = pltpu.get_barrier_semaphore()
+    for dev in [zp] + peers:
+        pl.semaphore_signal(barrier, inc=1, device_id=(tile, dev), device_id_type=MESH)
+    pl.semaphore_wait(barrier, half)
+
+    def block(g):
+        return out_ref.at[pl.ds(g * depth, depth)]
+
+    def copy(src, g, dev, slot):
+        return pltpu.make_async_remote_copy(
+            src_ref=src, dst_ref=block(g), send_sem=send_sem.at[slot],
+            recv_sem=recv_sem.at[g], device_id=(tile, dev), device_id_type=MESH,
+        )
+
+    sends = [copy(w_ref, me, zp, 0)]
+    sends[0].start()
+    for i, p in enumerate(peers):
+        c = copy(w_ref, me, p, 1 + i)
+        c.start()
+        sends.append(c)
+    block(me)[...] = w_ref[...]
+    copy(w_ref, zp, zp, 0).wait_recv()
+    for i, p in enumerate(peers):
+        c = copy(block(zp), zp, p, half + i)
+        c.start()
+        sends.append(c)
+    for p in peers:
+        copy(w_ref, p, p, 0).wait_recv()
+        copy(w_ref, lax.rem(p + half, groups), p, 0).wait_recv()
+    for c in sends:
+        c.wait_send()
+
+
+def gather_weights(weights):
+    groups = lax.axis_size("tm")
+    half = 4 if groups % 4 == 0 else groups // 2
+    depth = weights.shape[0]
+    return pl.pallas_call(
+        functools.partial(gather_kernel, half),
+        out_shape=jax.ShapeDtypeStruct((groups * depth,) + weights.shape[1:], weights.dtype),
+        in_specs=[pl.BlockSpec(memory_space=pltpu.VMEM)],
+        out_specs=pl.BlockSpec(memory_space=pltpu.VMEM),
+        scratch_shapes=[
+            pltpu.SemaphoreType.DMA((2 * half,)),
+            pltpu.SemaphoreType.DMA((groups,)),
+        ],
+        compiler_params=pltpu.CompilerParams(collective_id=0, has_side_effects=True),
+    )(weights)
+
+
 def on_device(controls, perturbations, owner, land_mask, diffusivity):
     rows = controls.shape[1]
     width = SWEEPS
@@ -47,7 +111,7 @@
         smooth = jnp.where(keep, weight_sweep(smooth, coef), 0.0)
     weights = smooth[:, width:width + rows].astype(jnp.bfloat16)
 
-    every = lax.all_gather(weights, "tm", axis=0, tiled=True)
+    every = gather_weights(weights)
     by_member = jnp.zeros_like(every).at[owner].set(every)
     member_count = owner.shape[0]
     factor = 1.0 / math.sqrt(member_count - 1)

time: 151 us -> 78.3 us (0.52)
  the two profiles are of different devices: /device:TPU:2 before, /device:TPU:6 now
where the time goes in v2:
time: 78.3 us; the launch traced here: 77.8 us
  Pallas kernels  35.5 us (45%)
  starting transfers between devices  27.8 us (36%)
  other arithmetic  9.28 us (12%)
  local copies, waits for them, and re-layouts  5.01 us (6%)
    pallas_call x1, Pallas kernels, gather_weights(): pl.pallas_call(functools.partial(gather_kernel, half), out_shape=jax.Shap...  35.5 us
    ppermute x2, starting transfers between devices, halo_rows(): after = lax.ppermute(head, 'tile', [(i + 1, i) for i in range(ends)])  24 us
    ppermute x2, starting transfers between devices, halo_rows(): before = lax.ppermute(tail, 'tile', [(i, i + 1) for i in range(ends)])  3.83 us
    dot_general x1, other arithmetic, on_device(): jnp.einsum('mvxly,mxly->vxly', perturbations[0], by_member, preferred_ele...  3.17 us
    scatter x1, local copies, waits for them, and re-layouts, on_device(): by_member = jnp.zeros_like(every).at[owner].set(every)  2.27 us
    slice x2, local copies, waits for them, and re-layouts, halo_rows(): lax.slice_in_dim(cells, cells.shape[dim] - width, cells.shape[dim], axis=...  1.79 us
  transfers between devices with their start and end apart: 4, of which 0 were waited for; matrix products, arithmetic and copies ran while one was open for 5% of the time, Pallas kernels for 0%

profile of v2, /device:TPU:6, one launch (start us, length us, event | category | flops | bytes accessed | tf_op | source)
XLA Modules:
  0.0 77.8 jit_solution(8134428719149789640)
XLA Ops:
  0.0 0.8 %fusion.59 = (s32[4,512]{1,0:T(4,128)S(1)}, s32[4,512]{1,0:T(4,128)S(1)}) fusion(s32[8,512]{1,0:T(8,128)} %param.8), kind=kLoop, calls=%fused_computation.93 | loop fusion | bytes 32768 | tf_op jit(solution)/shard_map/slice | solution.py:20
  0.8 1.9 %collective-permute-start.2 = (s32[4,512]{1,0:T(4,128)S(1)}, s32[4,512]{1,0:T(4,128)S(1)}, u32[]{:S(2)}, u32[]{:S(2)}) collective-permute-start(s32[4,512]{1,0:T(4,128)S(1)} %get-tuple-element.15), channel_id=1, source_target_pairs={{0,8},{8,16},{16,24},{24,32},{32,40},{40,48},{48,56},{56,64},{64,7... | collective-permute-start | bytes 24584 | tf_op jit(solution)/shard_map/ppermute | solution.py:21
  2.7 12.9 %collective-permute-start.3 = (s32[4,512]{1,0:T(4,128)S(1)}, s32[4,512]{1,0:T(4,128)S(1)}, u32[]{:S(2)}, u32[]{:S(2)}) collective-permute-start(s32[4,512]{1,0:T(4,128)S(1)} %get-tuple-element.16), channel_id=1, source_target_pairs={{8,0},{16,8},{24,16},{32,24},{40,32},{48,40},{56,48},{64,56},{72,6... | collective-permute-start | bytes 24584 | tf_op jit(solution)/shard_map/ppermute | solution.py:22
  15.6 1.0 %fusion.58 = (f32[2,4,8,512]{3,2,1,0:T(8,128)S(1)}, f32[2,4,8,512]{3,2,1,0:T(8,128)S(1)}) fusion(f32[2,8,8,512]{3,2,1,0:T(8,128)} %param.5), kind=kLoop, calls=%fused_computation.92 | loop fusion | bytes 524288 | tf_op jit(solution)/shard_map/slice | solution.py:20
  16.6 1.9 %collective-permute-start = (f32[2,4,8,512]{3,2,1,0:T(8,128)S(1)}, f32[2,4,8,512]{3,2,1,0:T(8,128)S(1)}, u32[]{:S(2)}, u32[]{:S(2)}) collective-permute-start(f32[2,4,8,512]{3,2,1,0:T(8,128)S(1)} %get-tuple-element.13), channel_id=1, source_target_pairs={{0,8},{8,16},{16,24},{24,32},{32,40},{40,48},{48,56},{56,64},{64,7... | collective-permute-start | bytes 393224 | tf_op jit(solution)/shard_map/ppermute | solution.py:21
  18.5 11.1 %collective-permute-start.1 = (f32[2,4,8,512]{3,2,1,0:T(8,128)S(1)}, f32[2,4,8,512]{3,2,1,0:T(8,128)S(1)}, u32[]{:S(2)}, u32[]{:S(2)}) collective-permute-start(f32[2,4,8,512]{3,2,1,0:T(8,128)S(1)} %get-tuple-element.14), channel_id=1, source_target_pairs={{8,0},{16,8},{24,16},{32,24},{40,32},{48,40},{56,48},{64,56},{72,6... | collective-permute-start | bytes 393224 | tf_op jit(solution)/shard_map/ppermute | solution.py:22
  29.7 0.8 slice_bitcast_fusion.1
  30.4 0.7 compare_select_fusion
  31.1 0.1 slice.128
  31.2 0.7 add_compare_fusion
  31.9 0.1 select_select_fusion
  32.0 0.2 fusion.45
  32.3 1.1 %maximum_select_fusion = f32[2,16,8,512]{3,2,1,0:T(8,128)S(1)} fusion(f32[2,4,8,512]{3,2,1,0:T(8,128)S(1)} %collective-permute-done.1, f32[2,8,8,512]{3,2,1,0:T(8,128)} %param.5, f32[2,4,8,512]{3,2,1,0:T(8,128)S(1)} %collective-permute-done, pred[16]{0:T(512)(128)(4,1)S(1)} %compare_and_fusion), kind=kLoop, calls=%fused_computation.63 | loop fusion | flops 393216 | bytes 1048592 | tf_op jit(solution)/shard_map/jit(_where)/select_n | solution.py:109
  33.4 0.4 fusion.6
  33.7 0.4 fusion.19
  34.1 0.4 fusion.32
  34.5 0.3 fusion.40
  34.9 0.8 fusion.56.w_ref
  35.6 35.5 %shard_map.55 = bf16[16,8,8,512]{3,2,1,0:T(8,128)(2,1)} custom-call(bf16[2,8,8,512]{3,2,1,0:T(8,128)(2,1)} %fusion.56.w_ref), custom_call_target="tpu_custom_call" | custom-call | tf_op jit(solution)/shard_map/pallas_call | solution.py:82
  71.1 0.1 broadcast_in_dim.96
  71.2 2.3 %scatter_fusion = bf16[16,8,8,512]{3,2,1,0:T(8,128)(2,1)S(1)} fusion(bf16[16,8,8,512]{3,2,1,0:T(8,128)(2,1)S(1)} %broadcast_in_dim.96, s32[16]{0:T(128)S(1)} %compare_select_fusion, bf16[16,8,8,512]{3,2,1,0:T(8,128)(2,1)} %shard_map.55), kind=kCustom, calls=%fused_computation | custom fusion | bytes 3145792 | tf_op jit(solution)/shard_map/scatter | solution.py:115
  73.5 0.3 bitcast_convert_fusion
  73.8 3.2 %multiply_reduce_fusion = f32[8,8,512,4]{2,1,0,3:T(8,128)S(1)} fusion(f32[8,8,512,16]{2,1,0,3:T(8,128)S(1)} %bitcast_convert_fusion, bf16[1,16,4,8,8,512]{5,4,3,2,1,0:T(8,128)(2,1)} %param.6), kind=kLoop, calls=%fused_computation.1 | loop fusion | flops 6160384 | bytes 6815744 | tf_op jit(solution)/shard_map/mvxly,mxly->vxly/dot_general | solution.py:118
  76.9 0.8 %multiply_bitcast_fusion = f32[1,4,8,8,512]{4,3,2,1,0:T(8,128)} fusion(f32[8,8,512,4]{2,1,0,3:T(8,128)S(1)} %multiply_reduce_fusion), kind=kLoop, calls=%fused_computation.64 | loop fusion | flops 131072 | bytes 1048576 | tf_op jit(solution)/shard_map/broadcast_in_dim | solution.py:121
  (7 shorter events, 0.0 us)
Async XLA Ops:
  0.8 30.4 %collective-permute-start.2 = (s32[4,512]{1,0:T(4,128)S(1)}, s32[4,512]{1,0:T(4,128)S(1)}, u32[]{:S(2)}, u32[]{:S(2)}) collective-permute-start(s32[4,512]{1,0:T(4,128)S(1)} %get-tuple-element.15), channel_id=1, source_target_pairs={{0,8},{8,16},{16,24},{24,32},{32,40},{40,48},{48,56},{56,64},{64,7... | collective-permute-start | bytes 24584 | tf_op jit(solution)/shard_map/ppermute | solution.py:21
  2.7 28.5 %collective-permute-start.3 = (s32[4,512]{1,0:T(4,128)S(1)}, s32[4,512]{1,0:T(4,128)S(1)}, u32[]{:S(2)}, u32[]{:S(2)}) collective-permute-start(s32[4,512]{1,0:T(4,128)S(1)} %get-tuple-element.16), channel_id=1, source_target_pairs={{8,0},{16,8},{24,16},{32,24},{40,32},{48,40},{56,48},{64,56},{72,6... | collective-permute-start | bytes 24584 | tf_op jit(solution)/shard_map/ppermute | solution.py:22
  16.6 15.7 %collective-permute-start = (f32[2,4,8,512]{3,2,1,0:T(8,128)S(1)}, f32[2,4,8,512]{3,2,1,0:T(8,128)S(1)}, u32[]{:S(2)}, u32[]{:S(2)}) collective-permute-start(f32[2,4,8,512]{3,2,1,0:T(8,128)S(1)} %get-tuple-element.13), channel_id=1, source_target_pairs={{0,8},{8,16},{16,24},{24,32},{32,40},{40,48},{48,56},{56,64},{64,7... | collective-permute-start | bytes 393224 | tf_op jit(solution)/shard_map/ppermute | solution.py:21
  18.5 13.8 %collective-permute-start.1 = (f32[2,4,8,512]{3,2,1,0:T(8,128)S(1)}, f32[2,4,8,512]{3,2,1,0:T(8,128)S(1)}, u32[]{:S(2)}, u32[]{:S(2)}) collective-permute-start(f32[2,4,8,512]{3,2,1,0:T(8,128)S(1)} %get-tuple-element.14), channel_id=1, source_target_pairs={{8,0},{16,8},{24,16},{32,24},{40,32},{48,40},{56,48},{64,56},{72,6... | collective-permute-start | bytes 393224 | tf_op jit(solution)/shard_map/ppermute | solution.py:22

commit v3 on v2

--- a/solution.py
+++ b/solution.py
@@ -11,16 +11,6 @@
 MESH = pl.DeviceIdType.MESH
 
 SWEEPS = 4
-
-
-def halo_rows(cells, width, dim):
-    count = lax.axis_size("tile")
-    ends = count - 1
-    head = lax.slice_in_dim(cells, 0, width, axis=dim)
-    tail = lax.slice_in_dim(cells, cells.shape[dim] - width, cells.shape[dim], axis=dim)
-    before = lax.ppermute(tail, "tile", [(i, i + 1) for i in range(ends)])
-    after = lax.ppermute(head, "tile", [(i + 1, i) for i in range(ends)])
-    return jnp.concatenate([before, cells, after], axis=dim)
 
 
 def weight_sweep(field, coef):
@@ -92,6 +82,55 @@
     )(weights)
 
 
+def halo_kernel(width, ctrl_ref, mask_ref, cb_ref, ca_ref, mb_ref, ma_ref, send_sem, recv_sem):
+    me = lax.axis_index("tile")
+    count = lax.axis_size("tile")
+    tm = lax.axis_index("tm")
+    rows = mask_ref.shape[0]
+    right = lax.rem(me + 1, count)
+    left = lax.rem(me + count - 1, count)
+
+    barrier = pltpu.get_barrier_semaphore()
+    for dev in (left, right):
+        pl.semaphore_signal(barrier, inc=1, device_id=(dev, tm), device_id_type=MESH)
+    pl.semaphore_wait(barrier, 2)
+
+    head, tail = pl.ds(0, width), pl.ds(rows - width, width)
+    plan = [
+        (ctrl_ref.at[:, tail], cb_ref, right),
+        (mask_ref.at[tail], mb_ref, right),
+        (ctrl_ref.at[:, head], ca_ref, left),
+        (mask_ref.at[head], ma_ref, left),
+    ]
+    copies = []
+    for i, (src, dst, dev) in enumerate(plan):
+        c = pltpu.make_async_remote_copy(
+            src_ref=src, dst_ref=dst, send_sem=send_sem.at[i], recv_sem=recv_sem.at[i],
+            device_id=(dev, tm), device_id_type=MESH,
+        )
+        c.start()
+        copies.append(c)
+    for c in copies:
+        c.wait_send()
+    for c in copies:
+        c.wait_recv()
+
+
+def exchange_halo(controls, land_mask, width):
+    slots, _, lev, ny = controls.shape
+    vmem = pl.BlockSpec(memory_space=pltpu.VMEM)
+    ctrl = jax.ShapeDtypeStruct((slots, width, lev, ny), controls.dtype)
+    mask = jax.ShapeDtypeStruct((width, ny), land_mask.dtype)
+    return pl.pallas_call(
+        functools.partial(halo_kernel, width),
+        out_shape=(ctrl, ctrl, mask, mask),
+        in_specs=[vmem, vmem],
+        out_specs=(vmem, vmem, vmem, vmem),
+        scratch_shapes=[pltpu.SemaphoreType.DMA((4,)), pltpu.SemaphoreType.DMA((4,))],
+        compiler_params=pltpu.CompilerParams(collective_id=1, has_side_effects=True),
+    )(controls, land_mask)
+
+
 def on_device(controls, perturbations, owner, land_mask, diffusivity):
     rows = controls.shape[1]
     width = SWEEPS
@@ -100,13 +139,14 @@
     grow = tile * rows - width + jnp.arange(rows + 2 * width)
     inside = (grow >= 0) & (grow < count * rows)
 
-    mask_wide = halo_rows(land_mask, width, 0)
+    cb, ca, mb, ma = exchange_halo(controls, land_mask, width)
+    mask_wide = jnp.concatenate([mb, land_mask, ma], axis=0)
     coef = jnp.where(
         mask_wide[:, None, :] == 1, diffusivity[1][None, :, None], diffusivity[0][None, :, None]
     )
     coef = jnp.where(inside[:, None, None], coef, 0.0)
     keep = inside[None, :, None, None]
-    smooth = jnp.where(keep, halo_rows(controls, width, 1), 0.0)
+    smooth = jnp.where(keep, jnp.concatenate([cb, controls, ca], axis=1), 0.0)
     for sweep_index in range(SWEEPS):
         smooth = jnp.where(keep, weight_sweep(smooth, coef), 0.0)
     weights = smooth[:, width:width + rows].astype(jnp.bfloat16)

time: 78.3 us -> 64.3 us (0.82)
  the two profiles are of different devices: /device:TPU:6 before, /device:TPU:1 now
where the time goes in v3:
time: 64.3 us; the launch traced here: 63.9 us
  Pallas kernels  51.8 us (81%)
  other arithmetic  8.75 us (14%)
  local copies, waits for them, and re-layouts  3.23 us (5%)
    pallas_call x1, Pallas kernels, gather_weights(): pl.pallas_call(functools.partial(gather_kernel, half), out_shape=jax.Shap...  34.2 us
    pallas_call x1, Pallas kernels, exchange_halo(): pl.pallas_call(functools.partial(halo_kernel, width), out_shape=(ctrl, ct...  17.7 us
    dot_general x1, other arithmetic, on_device(): jnp.einsum('mvxly,mxly->vxly', perturbations[0], by_member, preferred_ele...  3.17 us
    scatter x1, local copies, waits for them, and re-layouts, on_device(): by_member = jnp.zeros_like(every).at[owner].set(every)  2.27 us

profile of v3, /device:TPU:1, one launch (start us, length us, event | category | flops | bytes accessed | tf_op | source)
XLA Modules:
  0.0 63.9 jit_solution(13309252542360995589)
XLA Ops:
  0.0 17.7 %shard_map.55 = (f32[2,4,8,512]{3,2,1,0:T(8,128)}, f32[2,4,8,512]{3,2,1,0:T(8,128)}, s32[4,512]{1,0:T(4,128)}, s32[4,512]{1,0:T(4,128)}) custom-call(f32[2,8,8,512]{3,2,1,0:T(8,128)} %ctrl_ref.1, s32[8,512]{1,0:T(8,128)} %mask_ref.1), custom_call_target="tpu_custom_call" | custom-call | tf_op jit(solution)/shard_map/pallas_call | solution.py:124
  17.7 0.7 %add_compare_fusion = pred[16,512]{1,0:T(8,128)(4,1)S(1)} fusion(s32[4,512]{1,0:T(4,128)} %get-tuple-element.12, s32[8,512]{1,0:T(8,128)} %mask_ref.1, s32[4,512]{1,0:T(4,128)} %get-tuple-element.11), kind=kLoop, calls=%fused_computation.87 | loop fusion | flops 24576 | bytes 40960 | tf_op jit(solution)/shard_map/eq | solution.py:145
  18.4 0.8 %slice_bitcast_fusion.1 = (f32[8]{0:T(128)S(1)}, f32[8]{0:T(128)S(1)}) fusion(f32[2,8]{1,0:T(2,128)} %param.9), kind=kLoop, calls=%fused_computation.91 | loop fusion | bytes 128 | tf_op jit(solution)/shard_map/jit(_where)/broadcast_in_dim | solution.py:144
  19.2 0.1 select_select_fusion
  19.3 0.2 fusion.45
  19.5 1.2 %maximum_select_fusion = f32[2,16,8,512]{3,2,1,0:T(8,128)S(1)} fusion(f32[2,4,8,512]{3,2,1,0:T(8,128)} %get-tuple-element.10, f32[2,8,8,512]{3,2,1,0:T(8,128)} %ctrl_ref.1, f32[2,4,8,512]{3,2,1,0:T(8,128)} %get-tuple-element.9, pred[16]{0:T(512)(128)(4,1)S(1)} %compare_and_fusion), kind=kLoop, calls=%fused_computation.63 | loop fusion | flops 393216 | bytes 1048592 | tf_op jit(solution)/shard_map/jit(_where)/select_n | solution.py:149
  20.7 0.4 fusion.6
  21.1 0.4 fusion.19
  21.5 0.0 copy-start
  21.5 0.4 fusion.32
  21.9 0.3 fusion.40
  22.2 0.1 slice.112
  22.3 0.8 %fusion.56.w_ref = bf16[2,8,8,512]{3,2,1,0:T(8,128)(2,1)} fusion(f32[2,16,8,512]{3,2,1,0:T(8,128)S(1)} %get-tuple-element.16, f32[2,16,8,512]{3,2,1,0:T(8,128)S(1)} %fusion.32, f32[2,16,8,512]{3,2,1,0:T(8,128)S(1)} %get-tuple-element.14, f32[2,16,8,512]{3,2,1,0:T(8,128)S(1)} %get-tuple-element.15, f32[2,16,8,512]{3,2,1,0:T(8,128)S(1)} %get-tuple-element.13, ...), kind=kLoop, calls=%fused_computation.82 | loop fusion | flops 589824 | bytes 1703944 | tf_op jit(solution)/shard_map/convert
  23.1 34.2 %shard_map.56 = bf16[16,8,8,512]{3,2,1,0:T(8,128)(2,1)} custom-call(bf16[2,8,8,512]{3,2,1,0:T(8,128)(2,1)} %fusion.56.w_ref), custom_call_target="tpu_custom_call" | custom-call | tf_op jit(solution)/shard_map/pallas_call | solution.py:72
  57.2 0.0 copy-done
  57.3 0.1 broadcast_in_dim.96
  57.4 2.3 %scatter_fusion = bf16[16,8,8,512]{3,2,1,0:T(8,128)(2,1)S(1)} fusion(bf16[16,8,8,512]{3,2,1,0:T(8,128)(2,1)S(1)} %broadcast_in_dim.96, s32[16]{0:T(128)S(1)} %compare_select_fusion, bf16[16,8,8,512]{3,2,1,0:T(8,128)(2,1)} %shard_map.56), kind=kCustom, calls=%fused_computation | custom fusion | bytes 3145792 | tf_op jit(solution)/shard_map/scatter | solution.py:155
  59.6 0.3 bitcast_convert_fusion
  59.9 3.2 %multiply_reduce_fusion = f32[8,8,512,4]{2,1,0,3:T(8,128)S(1)} fusion(f32[8,8,512,16]{2,1,0,3:T(8,128)S(1)} %bitcast_convert_fusion, bf16[1,16,4,8,8,512]{5,4,3,2,1,0:T(8,128)(2,1)} %param.6), kind=kLoop, calls=%fused_computation.1 | loop fusion | flops 6160384 | bytes 6815744 | tf_op jit(solution)/shard_map/mvxly,mxly->vxly/dot_general | solution.py:158
  63.1 0.8 %multiply_bitcast_fusion = f32[1,4,8,8,512]{4,3,2,1,0:T(8,128)} fusion(f32[8,8,512,4]{2,1,0,3:T(8,128)S(1)} %multiply_reduce_fusion), kind=kLoop, calls=%fused_computation.64 | loop fusion | flops 131072 | bytes 1048576 | tf_op jit(solution)/shard_map/broadcast_in_dim | solution.py:161
  (4 shorter events, 0.0 us)
Async XLA Ops:
  21.5 35.8 %copy-start = (s32[16]{0:T(128)S(1)}, s32[16]{0:T(128)}, u32[]{:S(2)}) copy-start(s32[16]{0:T(128)} %param.7) | copy-start | bytes 196

commit v4 on v3

--- a/solution.py
+++ b/solution.py
@@ -23,7 +23,7 @@
     return field + flux
 
 
-def gather_kernel(half, w_ref, out_ref, send_sem, recv_sem):
+def gather_sum_kernel(half, factor, owner_ref, w_ref, pert_ref, out_ref, held, send_sem, recv_sem):
     tile = lax.axis_index("tile")
     me = lax.axis_index("tm")
     groups = lax.axis_size("tm")
@@ -38,7 +38,7 @@
     pl.semaphore_wait(barrier, half)
 
     def block(g):
-        return out_ref.at[pl.ds(g * depth, depth)]
+        return held.at[pl.ds(g * depth, depth)]
 
     def copy(src, g, dev, slot):
         return pltpu.make_async_remote_copy(
@@ -46,41 +46,56 @@
             recv_sem=recv_sem.at[g], device_id=(tile, dev), device_id_type=MESH,
         )
 
+    def add(src, g):
+        for k in range(depth):
+            member = owner_ref[g * depth + k]
+            out_ref[...] += pert_ref[member].astype(jnp.float32) * src[k].astype(jnp.float32)[None]
+
     sends = [copy(w_ref, me, zp, 0)]
     sends[0].start()
     for i, p in enumerate(peers):
         c = copy(w_ref, me, p, 1 + i)
         c.start()
         sends.append(c)
-    block(me)[...] = w_ref[...]
+    out_ref[...] = jnp.zeros(out_ref.shape, out_ref.dtype)
+    add(w_ref, me)
     copy(w_ref, zp, zp, 0).wait_recv()
     for i, p in enumerate(peers):
         c = copy(block(zp), zp, p, half + i)
         c.start()
         sends.append(c)
+    add(block(zp), zp)
     for p in peers:
         copy(w_ref, p, p, 0).wait_recv()
-        copy(w_ref, lax.rem(p + half, groups), p, 0).wait_recv()
+        add(block(p), p)
+        far = lax.rem(p + half, groups)
+        copy(w_ref, far, p, 0).wait_recv()
+        add(block(far), far)
     for c in sends:
         c.wait_send()
+    out_ref[...] = out_ref[...] * factor
 
 
-def gather_weights(weights):
+def gather_and_sum(owner, weights, pert):
     groups = lax.axis_size("tm")
     half = 4 if groups % 4 == 0 else groups // 2
     depth = weights.shape[0]
+    factor = 1.0 / math.sqrt(owner.shape[0] - 1)
+    vmem = pl.BlockSpec(memory_space=pltpu.VMEM)
     return pl.pallas_call(
-        functools.partial(gather_kernel, half),
-        out_shape=jax.ShapeDtypeStruct((groups * depth,) + weights.shape[1:], weights.dtype),
-        in_specs=[pl.BlockSpec(memory_space=pltpu.VMEM)],
-        out_specs=pl.BlockSpec(memory_space=pltpu.VMEM),
+        functools.partial(gather_sum_kernel, half, factor),
+        out_shape=jax.ShapeDtypeStruct(pert.shape[1:], jnp.float32),
+        in_specs=[pl.BlockSpec(memory_space=pltpu.SMEM), vmem, vmem],
+        out_specs=vmem,
         scratch_shapes=[
+            pltpu.VMEM((groups * depth,) + weights.shape[1:], weights.dtype),
             pltpu.SemaphoreType.DMA((2 * half,)),
             pltpu.SemaphoreType.DMA((groups,)),
         ],
-        compiler_params=pltpu.CompilerParams(collective_id=0, has_side_effects=True),
-    )(weights)
-
+        compiler_params=pltpu.CompilerParams(
+            collective_id=0, has_side_effects=True, vmem_limit_bytes=48 * 1024 * 1024
+        ),
+    )(owner, weights, pert)
 
 def halo_kernel(width, ctrl_ref, mask_ref, cb_ref, ca_ref, mb_ref, ma_ref, send_sem, recv_sem):
     me = lax.axis_index("tile")
@@ -151,14 +166,7 @@
         smooth = jnp.where(keep, weight_sweep(smooth, coef), 0.0)
     weights = smooth[:, width:width + rows].astype(jnp.bfloat16)
 
-    every = gather_weights(weights)
-    by_member = jnp.zeros_like(every).at[owner].set(every)
-    member_count = owner.shape[0]
-    factor = 1.0 / math.sqrt(member_count - 1)
-    summed = jnp.einsum(
-        "mvxly,mxly->vxly", perturbations[0], by_member, preferred_element_type=jnp.float32
-    )
-    return (summed * factor)[None]
+    return gather_and_sum(owner, weights, perturbations[0])[None]
 
 
 def solution(mesh):

time: 64.3 us -> 58.4 us (0.908)
  other arithmetic: 8.75 us -> 3.81 us
    dot_general x1 -> x0, other arithmetic: 3.17 us -> none  [on_device(): jnp.einsum('mvxly,mxly->vxly', perturbations[0], by_member, preferred_ele...]
    scatter x1 -> x0, local copies, waits for them, and re-layouts: 2.27 us -> none  [on_device(): by_member = jnp.zeros_like(every).at[owner].set(every)]
    unnamed x2 -> x5, local copies, waits for them, and re-layouts: 0.01 us -> 2.08 us
    broadcast_in_dim x1 -> x0, other arithmetic: 0.84 us -> none  [on_device(): return (summed * factor)[None]]
    another operation x1, other arithmetic: 0.76 us -> 0.11 us
where the time goes in v4:
time: 58.4 us; the launch traced here: 58.1 us
  Pallas kernels  51.2 us (88%)
  other arithmetic  3.81 us (7%)
  local copies, waits for them, and re-layouts  2.94 us (5%)
    pallas_call x1, Pallas kernels, gather_and_sum(): pl.pallas_call(functools.partial(gather_sum_kernel, half, factor), out_sh...  33.6 us
    pallas_call x1, Pallas kernels, exchange_halo(): pl.pallas_call(functools.partial(halo_kernel, width), out_shape=(ctrl, ct...  17.7 us
    unnamed x5, local copies, waits for them, and re-layouts  2.08 us

profile of v4, /device:TPU:1, one launch (start us, length us, event | category | flops | bytes accessed | tf_op | source)
XLA Modules:
  0.0 58.1 jit_solution(4542570263835361767)
XLA Ops:
  0.0 0.1 slice.112
  0.1 0.8 %slice_bitcast_fusion.1 = (f32[8]{0:T(128)S(1)}, f32[8]{0:T(128)S(1)}) fusion(f32[2,8]{1,0:T(2,128)} %param.9), kind=kLoop, calls=%fused_computation.86 | loop fusion | bytes 128 | tf_op jit(solution)/shard_map/jit(_where)/broadcast_in_dim | solution.py:159
  0.8 17.7 %shard_map.55 = (f32[2,4,8,512]{3,2,1,0:T(8,128)}, f32[2,4,8,512]{3,2,1,0:T(8,128)}, s32[4,512]{1,0:T(4,128)}, s32[4,512]{1,0:T(4,128)}) custom-call(f32[2,8,8,512]{3,2,1,0:T(8,128)} %ctrl_ref.1, s32[8,512]{1,0:T(8,128)} %mask_ref.1), custom_call_target="tpu_custom_call" | custom-call | tf_op jit(solution)/shard_map/pallas_call | solution.py:139
  18.5 0.7 %add_compare_fusion = pred[16,512]{1,0:T(8,128)(4,1)S(1)} fusion(s32[4,512]{1,0:T(4,128)} %get-tuple-element.12, s32[8,512]{1,0:T(8,128)} %mask_ref.1, s32[4,512]{1,0:T(4,128)} %get-tuple-element.11), kind=kLoop, calls=%fused_computation.83 | loop fusion | flops 24576 | bytes 40960 | tf_op jit(solution)/shard_map/eq | solution.py:160
  19.3 0.1 select_select_fusion
  19.4 1.2 %maximum_select_fusion = f32[2,16,8,512]{3,2,1,0:T(8,128)S(1)} fusion(f32[2,4,8,512]{3,2,1,0:T(8,128)} %get-tuple-element.10, f32[2,8,8,512]{3,2,1,0:T(8,128)} %ctrl_ref.1, f32[2,4,8,512]{3,2,1,0:T(8,128)} %get-tuple-element.9, pred[16]{0:T(512)(128)(4,1)S(1)} %compare_and_fusion), kind=kLoop, calls=%fused_computation.60 | loop fusion | flops 393216 | bytes 1048592 | tf_op jit(solution)/shard_map/jit(_where)/select_n | solution.py:164
  20.5 0.2 fusion.45
  20.7 0.4 fusion.6
  21.1 0.4 fusion.19
  21.5 0.0 copy-start
  21.5 0.0 copy-start.1
  21.5 0.4 fusion.32
  22.0 0.3 fusion.40
  22.3 0.1 fusion.56.w_ref
  22.4 1.3 %copy-done = bf16[1,16,4,8,8,512]{5,4,3,2,1,0:T(8,128)(2,1)S(1)} copy-done((bf16[1,16,4,8,8,512]{5,4,3,2,1,0:T(8,128)(2,1)S(1)}, bf16[1,16,4,8,8,512]{5,4,3,2,1,0:T(8,128)(2,1)}, u32[]{:S(2)}) %copy-start) | copy-done | bytes 4194328
  23.7 0.0 copy-done.1
  23.7 33.6 %shard_map.56 = f32[4,8,8,512]{3,2,1,0:T(8,128)S(1)} custom-call(s32[16]{0:T(128)S(1)} %copy-done.1, bf16[2,8,8,512]{3,2,1,0:T(8,128)(2,1)S(1)} %fusion.56.w_ref, bf16[16,4,8,8,512]{4,3,2,1,0:T(8,128)(2,1)S(1)} %bitcast.6), custom_call_target="tpu_custom_call" | custom-call | tf_op jit(solution)/shard_map/pallas_call | solution.py:85
  57.3 0.8 %copy.7 = f32[1,4,8,8,512]{4,3,2,1,0:T(8,128)} copy(f32[1,4,8,8,512]{4,3,2,1,0:T(8,128)S(1)} %bitcast.7) | data formatting | bytes 1048576
  (3 shorter events, 0.0 us)
Async XLA Ops:
  21.5 2.2 %copy-start = (bf16[1,16,4,8,8,512]{5,4,3,2,1,0:T(8,128)(2,1)S(1)}, bf16[1,16,4,8,8,512]{5,4,3,2,1,0:T(8,128)(2,1)}, u32[]{:S(2)}) copy-start(bf16[1,16,4,8,8,512]{5,4,3,2,1,0:T(8,128)(2,1)} %param.6) | copy-start | bytes 12582916
  21.5 2.2 %copy-start.1 = (s32[16]{0:T(128)S(1)}, s32[16]{0:T(128)}, u32[]{:S(2)}) copy-start(s32[16]{0:T(128)} %owner_ref.1) | copy-start | bytes 196

commit v5 on v1

v5 whole, which is shorter than its diff:
```python
import functools
import math

import jax
import jax.numpy as jnp
from jax import lax
from jax.experimental import pallas as pl
from jax.experimental.pallas import tpu as pltpu
from jax.sharding import PartitionSpec as P

MESH = pl.DeviceIdType.MESH

SWEEPS = 4


def lane_shifts(u):
    ny = u.shape[-1]
    lane = lax.broadcasted_iota(jnp.int32, u.shape, u.ndim - 1)
    fwd, back = pltpu.roll(u, 1, u.ndim - 1), pltpu.roll(u, ny - 1, u.ndim - 1)
    rolled = pltpu.roll(lane, 1, u.ndim - 1)
    moved = (rolled == lane - 1) | (rolled == lane + ny - 1)
    lower = jnp.where(moved, fwd, back)
    upper = jnp.where(moved, back, fwd)
    zero = jnp.zeros_like(u)
    return jnp.where(lane == 0, zero, lower), jnp.where(lane == ny - 1, zero, upper)


def row_shifts(u):
    zero = jnp.zeros_like(u[:1])
    return jnp.concatenate([zero, u[:-1]], axis=0), jnp.concatenate([u[1:], zero], axis=0)


def fused_kernel(half, width, factor, owner_ref, diff_ref, ctrl_ref, mask_ref, pert_hbm,
                 out_ref, ext, mext, held, pert, send_sem, recv_sem, pert_sem):
    tile = lax.axis_index("tile")
    count = lax.axis_size("tile")
    me = lax.axis_index("tm")
    groups = lax.axis_size("tm")
    depth, rows, lev, ny = ctrl_ref.shape
    wide = rows + 2 * width
    right = lax.rem(tile + 1, count)
    left = lax.rem(tile + count - 1, count)
    zp = lax.rem(me + half, groups)
    base = me - lax.rem(me, half)
    peers = [base + lax.rem(lax.rem(me, half) + d, half) for d in range(1, half)]

    load = pltpu.make_async_copy(pert_hbm, pert, pert_sem.at[0])
    load.start()

    barrier = pltpu.get_barrier_semaphore()
    for dev in ((left, me), (right, me), (tile, zp)) + tuple((tile, p) for p in peers):
        pl.semaphore_signal(barrier, inc=1, device_id=dev, device_id_type=MESH)
    pl.semaphore_wait(barrier, 2 + half)

    head, tail = pl.ds(0, width), pl.ds(rows - width, width)
    plan = [
        (ctrl_ref.at[:, tail], ext.at[:, pl.ds(0, width)], right),
        (mask_ref.at[tail], mext.at[pl.ds(0, width)], right),
        (ctrl_ref.at[:, head], ext.at[:, pl.ds(width + rows, width)], left),
        (mask_ref.at[head], mext.at[pl.ds(width + rows, width)], left),
    ]
    halo = []
    for i, (src, dst, dev) in enumerate(plan):
        c = pltpu.make_async_remote_copy(
            src_ref=src, dst_ref=dst, send_sem=send_sem.at[i], recv_sem=recv_sem.at[i],
            device_id=(dev, me), device_id_type=MESH,
        )
        c.start()
        halo.append(c)
    ext[:, pl.ds(width, rows)] = ctrl_ref[...]
    mext[pl.ds(width, rows)] = mask_ref[...]
    for c in halo:
        c.wait_recv()

    grow = tile * rows - width + lax.broadcasted_iota(jnp.int32, (wide, lev, ny), 0)
    inside = (grow >= 0) & (grow < count * rows)
    levels = lax.broadcasted_iota(jnp.int32, (wide, lev, ny), 1)
    sea = jnp.zeros((wide, lev, ny), jnp.float32)
    land = jnp.zeros((wide, lev, ny), jnp.float32)
    for l in range(lev):
        sea = jnp.where(levels == l, diff_ref[0, l], sea)
        land = jnp.where(levels == l, diff_ref[1, l], land)
    landed = jnp.broadcast_to(mext[...][:, None, :], (wide, lev, ny)) == 1
    coef = jnp.where(inside, jnp.where(landed, land, sea), 0.0)
    cxm, cxp = row_shifts(coef)
    cym, cyp = lane_shifts(coef)
    axm, axp = 0.5 * (coef + cxm), 0.5 * (coef + cxp)
    aym, ayp = 0.5 * (coef + cym), 0.5 * (coef + cyp)

    def block(g):
        return held.at[pl.ds(g * depth, depth)]

    for k in range(depth):
        u = jnp.where(inside, ext[k], 0.0)
        for sweep_index in range(SWEEPS):
            uxm, uxp = row_shifts(u)
            uym, uyp = lane_shifts(u)
            flux = axm * (uxm - u)
            flux = flux + axp * (uxp - u)
            flux = flux + aym * (uym - u)
            flux = flux + ayp * (uyp - u)
            u = jnp.where(inside, u + flux, 0.0)
        held[me * depth + k] = u[width:width + rows].astype(held.dtype)

    for c in halo:
        c.wait_send()

    def copy(src, g, dev, slot):
        return pltpu.make_async_remote_copy(
            src_ref=src, dst_ref=block(g), send_sem=send_sem.at[4 + slot],
            recv_sem=recv_sem.at[4 + g], device_id=(tile, dev), device_id_type=MESH,
        )

    def add(src, g):
        for k in range(depth):
            member = owner_ref[g * depth + k]
            out_ref[...] += pert[member].astype(jnp.float32) * src[k].astype(jnp.float32)[None]

    sends = []
    for i, p in enumerate([zp] + peers):
        c = copy(block(me), me, p, i)
        c.start()
        sends.append(c)
    out_ref[...] = jnp.zeros(out_ref.shape, out_ref.dtype)
    load.wait()
    add(block(me), me)
    copy(block(zp), zp, zp, 0).wait_recv()
    for i, p in enumerate(peers):
        c = copy(block(zp), zp, p, half + i)
        c.start()
        sends.append(c)
    add(block(zp), zp)
    for p in peers:
        copy(block(p), p, p, 0).wait_recv()
        add(block(p), p)
        far = lax.rem(p + half, groups)
        copy(block(far), far, p, 0).wait_recv()
        add(block(far), far)
    for c in sends:
        c.wait_send()
    out_ref[...] = out_ref[...] * factor


def on_device(controls, perturbations, owner, land_mask, diffusivity):
    groups = lax.axis_size("tm")
    half = 4 if groups % 4 == 0 else groups // 2
    depth, rows, lev, ny = controls.shape
    width = SWEEPS
    pert = perturbations[0]
    factor = 1.0 / math.sqrt(owner.shape[0] - 1)
    vmem = pl.BlockSpec(memory_space=pltpu.VMEM)
    smem = pl.BlockSpec(memory_space=pltpu.SMEM)
    out = pl.pallas_call(
        functools.partial(fused_kernel, half, width, factor),
        out_shape=jax.ShapeDtypeStruct(pert.shape[1:], jnp.float32),
        in_specs=[smem, smem, vmem, vmem, pl.BlockSpec(memory_space=pl.ANY)],
        out_specs=vmem,
        scratch_shapes=[
            pltpu.VMEM((depth, rows + 2 * width, lev, ny), controls.dtype),
            pltpu.VMEM((rows + 2 * width, ny), land_mask.dtype),
            pltpu.VMEM((groups * depth, rows, lev, ny), jnp.bfloat16),
            pltpu.VMEM(pert.shape, pert.dtype),
            pltpu.SemaphoreType.DMA((4 + 2 * half,)),
            pltpu.SemaphoreType.DMA((4 + groups,)),
            pltpu.SemaphoreType.DMA((1,)),
        ],
        compiler_params=pltpu.CompilerParams(
            collective_id=0, has_side_effects=True, vmem_limit_bytes=48 * 1024 * 1024
        ),
    )(owner, diffusivity, controls, land_mask, pert)
    return out[None]


def solution(mesh):
    return jax.shard_map(
        on_device,
        mesh=mesh,
        in_specs=(
            P("tm", "tile", None, None),
            P("tm", None, None, "tile", None, None),
            P(),
            P("tile", None),
            P(),
        ),
        out_specs=P("tm", None, "tile", None, None),
        check_vma=False,
    )
```

time: 151 us -> 53.1 us (0.35)
  the two profiles are of different devices: /device:TPU:2 before, /device:TPU:8 now
where the time goes in v5:
time: 53.1 us; the launch traced here: 52.9 us
  Pallas kernels  46.9 us (88%)
  local copies, waits for them, and re-layouts  5.98 us (11%)
    pallas_call x1, Pallas kernels, on_device(): pl.pallas_call(functools.partial(fused_kernel, half, width, factor), out_...  46.9 us
    unnamed x11, local copies, waits for them, and re-layouts  5.98 us

profile of v5, /device:TPU:8, one launch (start us, length us, event | category | flops | bytes accessed | tf_op | source)
XLA Modules:
  0.0 52.9 jit_solution(16980729790483595141)
XLA Ops:
  0.0 0.0 copy-start
  0.0 2.2 %copy-done = bf16[1,16,4,8,8,512]{5,4,3,2,1,0:T(8,128)(2,1)S(1)} copy-done((bf16[1,16,4,8,8,512]{5,4,3,2,1,0:T(8,128)(2,1)S(1)}, bf16[1,16,4,8,8,512]{5,4,3,2,1,0:T(8,128)(2,1)}, u32[]{:S(2)}) %copy-start) | copy-done | bytes 4194328
  2.2 0.0 copy-start.1
  2.2 0.9 %copy-done.1 = f32[2,8,8,512]{3,2,1,0:T(8,128)S(1)} copy-done((f32[2,8,8,512]{3,2,1,0:T(8,128)S(1)}, f32[2,8,8,512]{3,2,1,0:T(8,128)}, u32[]{:S(2)}) %copy-start.1) | copy-done | bytes 262168
  3.1 0.0 copy-start.2
  3.1 0.7 %copy-done.2 = s32[8,512]{1,0:T(8,128)S(1)} copy-done((s32[8,512]{1,0:T(8,128)S(1)}, s32[8,512]{1,0:T(8,128)}, u32[]{:S(2)}) %copy-start.2) | copy-done | bytes 16408
  3.9 0.0 copy-start.3
  3.9 0.7 %copy-done.3 = f32[2,8]{1,0:T(2,128)S(1)} copy-done((f32[2,8]{1,0:T(2,128)S(1)}, f32[2,8]{1,0:T(2,128)}, u32[]{:S(2)}) %copy-start.3) | copy-done | bytes 88
  4.5 0.0 copy-start.4
  4.5 0.7 %copy-done.4 = s32[16]{0:T(128)S(1)} copy-done((s32[16]{0:T(128)S(1)}, s32[16]{0:T(128)}, u32[]{:S(2)}) %copy-start.4) | copy-done | bytes 88
  5.2 46.9 %shard_map.55 = f32[4,8,8,512]{3,2,1,0:T(8,128)S(1)} custom-call(s32[16]{0:T(128)S(1)} %copy-done.4, f32[2,8]{1,0:T(2,128)S(1)} %copy-done.3, f32[2,8,8,512]{3,2,1,0:T(8,128)S(1)} %copy-done.1, s32[8,512]{1,0:T(8,128)S(1)} %copy-done.2, bf16[16,4,8,8,512]{4,3,2,1,0:T(8,128)(2,1)S(1)} %bitcast.2), custom_call_target="tpu_custom_call" | custom-call | tf_op jit(solution)/shard_map/pallas_call | solution.py:153
  52.1 0.8 %copy.7 = f32[1,4,8,8,512]{4,3,2,1,0:T(8,128)} copy(f32[1,4,8,8,512]{4,3,2,1,0:T(8,128)S(1)} %bitcast.3) | data formatting | bytes 1048576
Async XLA Ops:
  0.0 2.2 %copy-start = (bf16[1,16,4,8,8,512]{5,4,3,2,1,0:T(8,128)(2,1)S(1)}, bf16[1,16,4,8,8,512]{5,4,3,2,1,0:T(8,128)(2,1)}, u32[]{:S(2)}) copy-start(bf16[1,16,4,8,8,512]{5,4,3,2,1,0:T(8,128)(2,1)} %param.6) | copy-start | bytes 12582916
  2.2 0.9 %copy-start.1 = (f32[2,8,8,512]{3,2,1,0:T(8,128)S(1)}, f32[2,8,8,512]{3,2,1,0:T(8,128)}, u32[]{:S(2)}) copy-start(f32[2,8,8,512]{3,2,1,0:T(8,128)} %ctrl_ref.1) | copy-start | bytes 786436
  3.1 0.7 %copy-start.2 = (s32[8,512]{1,0:T(8,128)S(1)}, s32[8,512]{1,0:T(8,128)}, u32[]{:S(2)}) copy-start(s32[8,512]{1,0:T(8,128)} %mask_ref.1) | copy-start | bytes 49156
  3.9 0.7 %copy-start.3 = (f32[2,8]{1,0:T(2,128)S(1)}, f32[2,8]{1,0:T(2,128)}, u32[]{:S(2)}) copy-start(f32[2,8]{1,0:T(2,128)} %diff_ref.1) | copy-start | bytes 196
  4.5 0.7 %copy-start.4 = (s32[16]{0:T(128)S(1)}, s32[16]{0:T(128)}, u32[]{:S(2)}) copy-start(s32[16]{0:T(128)} %owner_ref.1) | copy-start | bytes 196

commit v6 on v5

--- a/solution.py
+++ b/solution.py
@@ -30,13 +30,14 @@
     return jnp.concatenate([zero, u[:-1]], axis=0), jnp.concatenate([u[1:], zero], axis=0)
 
 
-def fused_kernel(half, width, factor, owner_ref, diff_ref, ctrl_ref, mask_ref, pert_hbm,
-                 out_ref, ext, mext, held, pert, send_sem, recv_sem, pert_sem):
+def fused_kernel(half, width, factor, owner_hbm, diff_hbm, ctrl_hbm, mask_hbm, pert_hbm,
+                 out_ref, owner_ref, diff_ref, ctrl_ref, mask_ref, ext, mext, held, pert,
+                 send_sem, recv_sem, load_sem):
     tile = lax.axis_index("tile")
     count = lax.axis_size("tile")
     me = lax.axis_index("tm")
     groups = lax.axis_size("tm")
-    depth, rows, lev, ny = ctrl_ref.shape
+    depth, rows, lev, ny = ctrl_hbm.shape
     wide = rows + 2 * width
     right = lax.rem(tile + 1, count)
     left = lax.rem(tile + count - 1, count)
@@ -44,8 +45,17 @@
     base = me - lax.rem(me, half)
     peers = [base + lax.rem(lax.rem(me, half) + d, half) for d in range(1, half)]
 
-    load = pltpu.make_async_copy(pert_hbm, pert, pert_sem.at[0])
-    load.start()
+    loads = [
+        pltpu.make_async_copy(src, dst, load_sem.at[i])
+        for i, (src, dst) in enumerate(
+            [(ctrl_hbm, ctrl_ref), (mask_hbm, mask_ref), (diff_hbm, diff_ref),
+             (owner_hbm, owner_ref), (pert_hbm, pert)]
+        )
+    ]
+    for c in loads:
+        c.start()
+    for c in loads[:4]:
+        c.wait()
 
     barrier = pltpu.get_barrier_semaphore()
     for dev in ((left, me), (right, me), (tile, zp)) + tuple((tile, p) for p in peers):
@@ -122,7 +132,7 @@
         c.start()
         sends.append(c)
     out_ref[...] = jnp.zeros(out_ref.shape, out_ref.dtype)
-    load.wait()
+    loads[4].wait()
     add(block(me), me)
     copy(block(zp), zp, zp, 0).wait_recv()
     for i, p in enumerate(peers):
@@ -149,23 +159,27 @@
     pert = perturbations[0]
     factor = 1.0 / math.sqrt(owner.shape[0] - 1)
     vmem = pl.BlockSpec(memory_space=pltpu.VMEM)
-    smem = pl.BlockSpec(memory_space=pltpu.SMEM)
+    hbm = pl.BlockSpec(memory_space=pl.ANY)
     out = pl.pallas_call(
         functools.partial(fused_kernel, half, width, factor),
         out_shape=jax.ShapeDtypeStruct(pert.shape[1:], jnp.float32),
-        in_specs=[smem, smem, vmem, vmem, pl.BlockSpec(memory_space=pl.ANY)],
+        in_specs=[hbm] * 5,
         out_specs=vmem,
         scratch_shapes=[
+            pltpu.SMEM(owner.shape, owner.dtype),
+            pltpu.SMEM(diffusivity.shape, diffusivity.dtype),
+            pltpu.VMEM(controls.shape, controls.dtype),
+            pltpu.VMEM(land_mask.shape, land_mask.dtype),
             pltpu.VMEM((depth, rows + 2 * width, lev, ny), controls.dtype),
             pltpu.VMEM((rows + 2 * width, ny), land_mask.dtype),
             pltpu.VMEM((groups * depth, rows, lev, ny), jnp.bfloat16),
             pltpu.VMEM(pert.shape, pert.dtype),
             pltpu.SemaphoreType.DMA((4 + 2 * half,)),
             pltpu.SemaphoreType.DMA((4 + groups,)),
-            pltpu.SemaphoreType.DMA((1,)),
+            pltpu.SemaphoreType.DMA((5,)),
         ],
         compiler_params=pltpu.CompilerParams(
-            collective_id=0, has_side_effects=True, vmem_limit_bytes=48 * 1024 * 1024
+            collective_id=0, has_side_effects=True, vmem_limit_bytes=64 * 1024 * 1024
         ),
     )(owner, diffusivity, controls, land_mask, pert)
     return out[None]

time: 53.1 us -> 49.8 us (0.938)
  local copies, waits for them, and re-layouts: 5.98 us -> 1.87 us
  Pallas kernels: 46.9 us -> 47.7 us
    unnamed x11 -> x1, local copies, waits for them, and re-layouts: 5.98 us -> 1.87 us
    pallas_call x1, Pallas kernels: 46.9 us -> 47.7 us  [on_device(): pl.pallas_call(functools.partial(fused_kernel, half, width, factor), out_...]
where the time goes in v6:
time: 49.8 us; the launch traced here: 49.6 us
  Pallas kernels  47.7 us (96%)
  local copies, waits for them, and re-layouts  1.87 us (4%)
    pallas_call x1, Pallas kernels, on_device(): pl.pallas_call(functools.partial(fused_kernel, half, width, factor), out_...  47.7 us
    unnamed x1, local copies, waits for them, and re-layouts  1.87 us

profile of v6, /device:TPU:8, one launch (start us, length us, event | category | flops | bytes accessed | tf_op | source)
XLA Modules:
  0.0 49.6 jit_solution(475421013372153901)
XLA Ops:
  0.0 47.7 %shard_map.55 = f32[4,8,8,512]{3,2,1,0:T(8,128)} custom-call(s32[16]{0:T(128)} %owner_hbm.1, f32[2,8]{1,0:T(2,128)} %diff_hbm.1, f32[2,8,8,512]{3,2,1,0:T(8,128)} %ctrl_hbm.1, s32[8,512]{1,0:T(8,128)} %mask_hbm.1, bf16[16,4,8,8,512]{4,3,2,1,0:T(8,128)(2,1)} %bitcast.2), custom_call_target="tpu_custom_call" | custom-call | tf_op jit(solution)/shard_map/pallas_call | solution.py:163
  47.7 1.9 %copy.7 = f32[1,4,8,8,512]{4,3,2,1,0:T(8,128)} copy(f32[1,4,8,8,512]{4,3,2,1,0:T(8,128)} %bitcast.3) | data formatting | bytes 1048576

commit v7 on v6

--- a/solution.py
+++ b/solution.py
@@ -97,9 +97,20 @@
     axm, axp = 0.5 * (coef + cxm), 0.5 * (coef + cxp)
     aym, ayp = 0.5 * (coef + cym), 0.5 * (coef + cyp)
 
-    def block(g):
-        return held.at[pl.ds(g * depth, depth)]
-
+    def slot(g, k):
+        return held.at[pl.ds(g * depth + k, 1)]
+
+    def copy(g, k, dev, sem):
+        return pltpu.make_async_remote_copy(
+            src_ref=slot(g, k), dst_ref=slot(g, k), send_sem=send_sem.at[sem],
+            recv_sem=recv_sem.at[4 + g * depth + k], device_id=(tile, dev), device_id_type=MESH,
+        )
+
+    def add(g, k):
+        member = owner_ref[g * depth + k]
+        out_ref[...] += pert[member].astype(jnp.float32) * held[g * depth + k].astype(jnp.float32)[None]
+
+    sends = []
     for k in range(depth):
         u = jnp.where(inside, ext[k], 0.0)
         for sweep_index in range(SWEEPS):
@@ -111,41 +122,29 @@
             flux = flux + ayp * (uyp - u)
             u = jnp.where(inside, u + flux, 0.0)
         held[me * depth + k] = u[width:width + rows].astype(held.dtype)
+        for i, p in enumerate([zp] + peers):
+            c = copy(me, k, p, 4 + k * 2 * half + i)
+            c.start()
+            sends.append(c)
 
     for c in halo:
         c.wait_send()
-
-    def copy(src, g, dev, slot):
-        return pltpu.make_async_remote_copy(
-            src_ref=src, dst_ref=block(g), send_sem=send_sem.at[4 + slot],
-            recv_sem=recv_sem.at[4 + g], device_id=(tile, dev), device_id_type=MESH,
-        )
-
-    def add(src, g):
-        for k in range(depth):
-            member = owner_ref[g * depth + k]
-            out_ref[...] += pert[member].astype(jnp.float32) * src[k].astype(jnp.float32)[None]
-
-    sends = []
-    for i, p in enumerate([zp] + peers):
-        c = copy(block(me), me, p, i)
-        c.start()
-        sends.append(c)
     out_ref[...] = jnp.zeros(out_ref.shape, out_ref.dtype)
     loads[4].wait()
-    add(block(me), me)
-    copy(block(zp), zp, zp, 0).wait_recv()
-    for i, p in enumerate(peers):
-        c = copy(block(zp), zp, p, half + i)
-        c.start()
-        sends.append(c)
-    add(block(zp), zp)
+    for k in range(depth):
+        add(me, k)
+    for k in range(depth):
+        copy(zp, k, zp, 4).wait_recv()
+        for i, p in enumerate(peers):
+            c = copy(zp, k, p, 4 + k * 2 * half + half + i)
+            c.start()
+            sends.append(c)
+        add(zp, k)
     for p in peers:
-        copy(block(p), p, p, 0).wait_recv()
-        add(block(p), p)
-        far = lax.rem(p + half, groups)
-        copy(block(far), far, p, 0).wait_recv()
-        add(block(far), far)
+        for g in (p, lax.rem(p + half, groups)):
+            for k in range(depth):
+                copy(g, k, p, 4).wait_recv()
+                add(g, k)
     for c in sends:
         c.wait_send()
     out_ref[...] = out_ref[...] * factor
@@ -174,8 +173,8 @@
             pltpu.VMEM((rows + 2 * width, ny), land_mask.dtype),
             pltpu.VMEM((groups * depth, rows, lev, ny), jnp.bfloat16),
             pltpu.VMEM(pert.shape, pert.dtype),
-            pltpu.SemaphoreType.DMA((4 + 2 * half,)),
-            pltpu.SemaphoreType.DMA((4 + groups,)),
+            pltpu.SemaphoreType.DMA((4 + 2 * half * depth,)),
+            pltpu.SemaphoreType.DMA((4 + groups * depth,)),
             pltpu.SemaphoreType.DMA((5,)),
         ],
         compiler_params=pltpu.CompilerParams(

time: 49.8 us -> 47 us (0.944)
  Pallas kernels: 47.7 us -> 44.9 us
    pallas_call x1, Pallas kernels: 47.7 us -> 44.9 us  [on_device(): pl.pallas_call(functools.partial(fused_kernel, half, width, factor), out_...]
where the time goes in v7:
time: 47 us; the launch traced here: 46.8 us
  Pallas kernels  44.9 us (96%)
  local copies, waits for them, and re-layouts  1.87 us (4%)
    pallas_call x1, Pallas kernels, on_device(): pl.pallas_call(functools.partial(fused_kernel, half, width, factor), out_...  44.9 us
    unnamed x1, local copies, waits for them, and re-layouts  1.87 us

profile of v7, /device:TPU:8, one launch (start us, length us, event | category | flops | bytes accessed | tf_op | source)
XLA Modules:
  0.0 46.8 jit_solution(10137427906232182397)
XLA Ops:
  0.0 44.9 %shard_map.55 = f32[4,8,8,512]{3,2,1,0:T(8,128)} custom-call(s32[16]{0:T(128)} %owner_hbm.1, f32[2,8]{1,0:T(2,128)} %diff_hbm.1, f32[2,8,8,512]{3,2,1,0:T(8,128)} %ctrl_hbm.1, s32[8,512]{1,0:T(8,128)} %mask_hbm.1, bf16[16,4,8,8,512]{4,3,2,1,0:T(8,128)(2,1)} %bitcast.2), custom_call_target="tpu_custom_call" | custom-call | tf_op jit(solution)/shard_map/pallas_call | solution.py:162
  45.0 1.9 %copy.7 = f32[1,4,8,8,512]{4,3,2,1,0:T(8,128)} copy(f32[1,4,8,8,512]{4,3,2,1,0:T(8,128)} %bitcast.3) | data formatting | bytes 1048576

commit v8 on v7

--- a/solution.py
+++ b/solution.py
@@ -23,11 +23,6 @@
     upper = jnp.where(moved, back, fwd)
     zero = jnp.zeros_like(u)
     return jnp.where(lane == 0, zero, lower), jnp.where(lane == ny - 1, zero, upper)
-
-
-def row_shifts(u):
-    zero = jnp.zeros_like(u[:1])
-    return jnp.concatenate([zero, u[:-1]], axis=0), jnp.concatenate([u[1:], zero], axis=0)
 
 
 def fused_kernel(half, width, factor, owner_hbm, diff_hbm, ctrl_hbm, mask_hbm, pert_hbm,
@@ -92,10 +87,11 @@
         land = jnp.where(levels == l, diff_ref[1, l], land)
     landed = jnp.broadcast_to(mext[...][:, None, :], (wide, lev, ny)) == 1
     coef = jnp.where(inside, jnp.where(landed, land, sea), 0.0)
-    cxm, cxp = row_shifts(coef)
-    cym, cyp = lane_shifts(coef)
-    axm, axp = 0.5 * (coef + cxm), 0.5 * (coef + cxp)
-    aym, ayp = 0.5 * (coef + cym), 0.5 * (coef + cyp)
+    mid = coef[1:-1]
+    cym, cyp = lane_shifts(mid)
+    axm, axp = 0.5 * (mid + coef[:-2]), 0.5 * (mid + coef[2:])
+    aym, ayp = 0.5 * (mid + cym), 0.5 * (mid + cyp)
+    kept = inside[1:-1]
 
     def slot(g, k):
         return held.at[pl.ds(g * depth + k, 1)]
@@ -114,14 +110,15 @@
     for k in range(depth):
         u = jnp.where(inside, ext[k], 0.0)
         for sweep_index in range(SWEEPS):
-            uxm, uxp = row_shifts(u)
-            uym, uyp = lane_shifts(u)
-            flux = axm * (uxm - u)
-            flux = flux + axp * (uxp - u)
-            flux = flux + aym * (uym - u)
-            flux = flux + ayp * (uyp - u)
-            u = jnp.where(inside, u + flux, 0.0)
-        held[me * depth + k] = u[width:width + rows].astype(held.dtype)
+            lo, hi = sweep_index, wide - 2 - sweep_index
+            centre = u[1:-1]
+            uym, uyp = lane_shifts(centre)
+            flux = axm[lo:hi] * (u[:-2] - centre)
+            flux = flux + axp[lo:hi] * (u[2:] - centre)
+            flux = flux + aym[lo:hi] * (uym - centre)
+            flux = flux + ayp[lo:hi] * (uyp - centre)
+            u = jnp.where(kept[lo:hi], centre + flux, 0.0)
+        held[me * depth + k] = u.astype(held.dtype)
         for i, p in enumerate([zp] + peers):
             c = copy(me, k, p, 4 + k * 2 * half + i)
             c.start()

time: 47 us -> 47 us (level)
  no operation moved by 1% of the time
where the time goes in v8:
time: 47 us; the launch traced here: 46.8 us
  Pallas kernels  44.9 us (96%)
  local copies, waits for them, and re-layouts  1.87 us (4%)
    pallas_call x1, Pallas kernels, on_device(): pl.pallas_call(functools.partial(fused_kernel, half, width, factor), out_...  44.9 us
    unnamed x1, local copies, waits for them, and re-layouts  1.87 us

profile of v8, /device:TPU:8, one launch (start us, length us, event | category | flops | bytes accessed | tf_op | source)
XLA Modules:
  0.0 46.8 jit_solution(10137427906232182397)
XLA Ops:
  0.0 44.9 %shard_map.55 = f32[4,8,8,512]{3,2,1,0:T(8,128)} custom-call(s32[16]{0:T(128)} %owner_hbm.1, f32[2,8]{1,0:T(2,128)} %diff_hbm.1, f32[2,8,8,512]{3,2,1,0:T(8,128)} %ctrl_hbm.1, s32[8,512]{1,0:T(8,128)} %mask_hbm.1, bf16[16,4,8,8,512]{4,3,2,1,0:T(8,128)(2,1)} %bitcast.2), custom_call_target="tpu_custom_call" | custom-call | tf_op jit(solution)/shard_map/pallas_call | solution.py:159
  45.0 1.9 %copy.7 = f32[1,4,8,8,512]{4,3,2,1,0:T(8,128)} copy(f32[1,4,8,8,512]{4,3,2,1,0:T(8,128)} %bitcast.3) | data formatting | bytes 1048576

commit v9 on v8

--- a/solution.py
+++ b/solution.py
@@ -34,6 +34,7 @@
     groups = lax.axis_size("tm")
     depth, rows, lev, ny = ctrl_hbm.shape
     wide = rows + 2 * width
+    nhalo = 2 + 2 * depth
     right = lax.rem(tile + 1, count)
     left = lax.rem(tile + count - 1, count)
     zp = lax.rem(me + half, groups)
@@ -58,12 +59,14 @@
     pl.semaphore_wait(barrier, 2 + half)
 
     head, tail = pl.ds(0, width), pl.ds(rows - width, width)
+    before, after = pl.ds(0, width), pl.ds(width + rows, width)
     plan = [
-        (ctrl_ref.at[:, tail], ext.at[:, pl.ds(0, width)], right),
-        (mask_ref.at[tail], mext.at[pl.ds(0, width)], right),
-        (ctrl_ref.at[:, head], ext.at[:, pl.ds(width + rows, width)], left),
-        (mask_ref.at[head], mext.at[pl.ds(width + rows, width)], left),
+        (mask_ref.at[tail], mext.at[before], right),
+        (mask_ref.at[head], mext.at[after], left),
     ]
+    for k in range(depth):
+        plan.append((ctrl_ref.at[k, tail], ext.at[k, before], right))
+        plan.append((ctrl_ref.at[k, head], ext.at[k, after], left))
     halo = []
     for i, (src, dst, dev) in enumerate(plan):
         c = pltpu.make_async_remote_copy(
@@ -74,7 +77,7 @@
         halo.append(c)
     ext[:, pl.ds(width, rows)] = ctrl_ref[...]
     mext[pl.ds(width, rows)] = mask_ref[...]
-    for c in halo:
+    for c in halo[:2]:
         c.wait_recv()
 
     grow = tile * rows - width + lax.broadcasted_iota(jnp.int32, (wide, lev, ny), 0)
@@ -99,7 +102,7 @@
     def copy(g, k, dev, sem):
         return pltpu.make_async_remote_copy(
             src_ref=slot(g, k), dst_ref=slot(g, k), send_sem=send_sem.at[sem],
-            recv_sem=recv_sem.at[4 + g * depth + k], device_id=(tile, dev), device_id_type=MESH,
+            recv_sem=recv_sem.at[nhalo + g * depth + k], device_id=(tile, dev), device_id_type=MESH,
         )
 
     def add(g, k):
@@ -108,6 +111,8 @@
 
     sends = []
     for k in range(depth):
+        for c in halo[2 + 2 * k:4 + 2 * k]:
+            c.wait_recv()
         u = jnp.where(inside, ext[k], 0.0)
         for sweep_index in range(SWEEPS):
             lo, hi = sweep_index, wide - 2 - sweep_index
@@ -120,7 +125,7 @@
             u = jnp.where(kept[lo:hi], centre + flux, 0.0)
         held[me * depth + k] = u.astype(held.dtype)
         for i, p in enumerate([zp] + peers):
-            c = copy(me, k, p, 4 + k * 2 * half + i)
+            c = copy(me, k, p, nhalo + k * 2 * half + i)
             c.start()
             sends.append(c)
 
@@ -131,16 +136,16 @@
     for k in range(depth):
         add(me, k)
     for k in range(depth):
-        copy(zp, k, zp, 4).wait_recv()
+        copy(zp, k, zp, nhalo).wait_recv()
         for i, p in enumerate(peers):
-            c = copy(zp, k, p, 4 + k * 2 * half + half + i)
+            c = copy(zp, k, p, nhalo + k * 2 * half + half + i)
             c.start()
             sends.append(c)
         add(zp, k)
     for p in peers:
         for g in (p, lax.rem(p + half, groups)):
             for k in range(depth):
-                copy(g, k, p, 4).wait_recv()
+                copy(g, k, p, nhalo).wait_recv()
                 add(g, k)
     for c in sends:
         c.wait_send()
@@ -170,8 +175,8 @@
             pltpu.VMEM((rows + 2 * width, ny), land_mask.dtype),
             pltpu.VMEM((groups * depth, rows, lev, ny), jnp.bfloat16),
             pltpu.VMEM(pert.shape, pert.dtype),
-            pltpu.SemaphoreType.DMA((4 + 2 * half * depth,)),
-            pltpu.SemaphoreType.DMA((4 + groups * depth,)),
+            pltpu.SemaphoreType.DMA((2 + 2 * depth + 2 * half * depth,)),
+            pltpu.SemaphoreType.DMA((2 + 2 * depth + groups * depth,)),
             pltpu.SemaphoreType.DMA((5,)),
         ],
         compiler_params=pltpu.CompilerParams(

time: 47 us -> 43.7 us (0.930)
  the two profiles are of different devices: /device:TPU:8 before, /device:TPU:38 now
where the time goes in v9:
time: 43.7 us; the launch traced here: 43.6 us
  Pallas kernels  41.7 us (95%)
  local copies, waits for them, and re-layouts  1.87 us (4%)
    pallas_call x1, Pallas kernels, on_device(): pl.pallas_call(functools.partial(fused_kernel, half, width, factor), out_...  41.7 us
    unnamed x1, local copies, waits for them, and re-layouts  1.87 us

profile of v9, /device:TPU:38, one launch (start us, length us, event | category | flops | bytes accessed | tf_op | source)
XLA Modules:
  0.0 43.6 jit_solution(15715298094316633944)
XLA Ops:
  0.0 41.7 %shard_map.55 = f32[4,8,8,512]{3,2,1,0:T(8,128)} custom-call(s32[16]{0:T(128)} %owner_hbm.1, f32[2,8]{1,0:T(2,128)} %diff_hbm.1, f32[2,8,8,512]{3,2,1,0:T(8,128)} %ctrl_hbm.1, s32[8,512]{1,0:T(8,128)} %mask_hbm.1, bf16[16,4,8,8,512]{4,3,2,1,0:T(8,128)(2,1)} %bitcast.2), custom_call_target="tpu_custom_call" | custom-call | tf_op jit(solution)/shard_map/pallas_call | solution.py:164
  41.7 1.9 %copy.7 = f32[1,4,8,8,512]{4,3,2,1,0:T(8,128)} copy(f32[1,4,8,8,512]{4,3,2,1,0:T(8,128)} %bitcast.3) | data formatting | bytes 1048576

commit v10 on v9

--- a/solution.py
+++ b/solution.py
@@ -77,45 +77,30 @@
         halo.append(c)
     ext[:, pl.ds(width, rows)] = ctrl_ref[...]
     mext[pl.ds(width, rows)] = mask_ref[...]
-    for c in halo[:2]:
-        c.wait_recv()
-
-    grow = tile * rows - width + lax.broadcasted_iota(jnp.int32, (wide, lev, ny), 0)
-    inside = (grow >= 0) & (grow < count * rows)
-    levels = lax.broadcasted_iota(jnp.int32, (wide, lev, ny), 1)
-    sea = jnp.zeros((wide, lev, ny), jnp.float32)
-    land = jnp.zeros((wide, lev, ny), jnp.float32)
+    hr = rows // 2
+    win = hr + 2 * width
+    levels = lax.broadcasted_iota(jnp.int32, (win, lev, ny), 1)
+    sea = jnp.zeros((win, lev, ny), jnp.float32)
+    land = jnp.zeros((win, lev, ny), jnp.float32)
     for l in range(lev):
         sea = jnp.where(levels == l, diff_ref[0, l], sea)
         land = jnp.where(levels == l, diff_ref[1, l], land)
-    landed = jnp.broadcast_to(mext[...][:, None, :], (wide, lev, ny)) == 1
-    coef = jnp.where(inside, jnp.where(landed, land, sea), 0.0)
-    mid = coef[1:-1]
-    cym, cyp = lane_shifts(mid)
-    axm, axp = 0.5 * (mid + coef[:-2]), 0.5 * (mid + coef[2:])
-    aym, ayp = 0.5 * (mid + cym), 0.5 * (mid + cyp)
-    kept = inside[1:-1]
-
-    def slot(g, k):
-        return held.at[pl.ds(g * depth + k, 1)]
-
-    def copy(g, k, dev, sem):
-        return pltpu.make_async_remote_copy(
-            src_ref=slot(g, k), dst_ref=slot(g, k), send_sem=send_sem.at[sem],
-            recv_sem=recv_sem.at[nhalo + g * depth + k], device_id=(tile, dev), device_id_type=MESH,
-        )
-
-    def add(g, k):
-        member = owner_ref[g * depth + k]
-        out_ref[...] += pert[member].astype(jnp.float32) * held[g * depth + k].astype(jnp.float32)[None]
-
-    sends = []
-    for k in range(depth):
-        for c in halo[2 + 2 * k:4 + 2 * k]:
-            c.wait_recv()
-        u = jnp.where(inside, ext[k], 0.0)
+
+    def prep(h):
+        grow = tile * rows - width + h * hr + lax.broadcasted_iota(jnp.int32, (win, lev, ny), 0)
+        inside = (grow >= 0) & (grow < count * rows)
+        landed = jnp.broadcast_to(mext[pl.ds(h * hr, win)][:, None, :], (win, lev, ny)) == 1
+        coef = jnp.where(inside, jnp.where(landed, land, sea), 0.0)
+        mid = coef[1:-1]
+        cym, cyp = lane_shifts(mid)
+        return (inside, inside[1:-1], 0.5 * (mid + coef[:-2]), 0.5 * (mid + coef[2:]),
+                0.5 * (mid + cym), 0.5 * (mid + cyp))
+
+    def smooth(k, h, prepped):
+        inside, kept, axm, axp, aym, ayp = prepped
+        u = jnp.where(inside, ext[k, pl.ds(h * hr, win)], 0.0)
         for sweep_index in range(SWEEPS):
-            lo, hi = sweep_index, wide - 2 - sweep_index
+            lo, hi = sweep_index, win - 2 - sweep_index
             centre = u[1:-1]
             uym, uyp = lane_shifts(centre)
             flux = axm[lo:hi] * (u[:-2] - centre)
@@ -123,34 +108,69 @@
             flux = flux + aym[lo:hi] * (uym - centre)
             flux = flux + ayp[lo:hi] * (uyp - centre)
             u = jnp.where(kept[lo:hi], centre + flux, 0.0)
-        held[me * depth + k] = u.astype(held.dtype)
-        for i, p in enumerate([zp] + peers):
-            c = copy(me, k, p, nhalo + k * 2 * half + i)
-            c.start()
-            sends.append(c)
-
-    for c in halo:
-        c.wait_send()
-    out_ref[...] = jnp.zeros(out_ref.shape, out_ref.dtype)
-    loads[4].wait()
-    for k in range(depth):
-        add(me, k)
-    for k in range(depth):
-        copy(zp, k, zp, nhalo).wait_recv()
-        for i, p in enumerate(peers):
-            c = copy(zp, k, p, nhalo + k * 2 * half + half + i)
-            c.start()
-            sends.append(c)
-        add(zp, k)
-    for p in peers:
-        for g in (p, lax.rem(p + half, groups)):
+        held[me * depth + k, pl.ds(h * hr, hr)] = u.astype(held.dtype)
+
+    per = 2 * half - 1
+
+    def copy(g, k, h, dev, sem):
+        piece = held.at[pl.ds(g * depth + k, 1), pl.ds(h * hr, hr)]
+        return pltpu.make_async_remote_copy(
+            src_ref=piece, dst_ref=piece, send_sem=send_sem.at[nhalo + (k * 2 + h) * per + sem],
+            recv_sem=recv_sem.at[nhalo + (g * depth + k) * 2 + h],
+            device_id=(tile, dev), device_id_type=MESH,
+        )
+
+    def add(g, k):
+        member = owner_ref[g * depth + k]
+        out_ref[...] += pert[member].astype(jnp.float32) * held[g * depth + k].astype(jnp.float32)[None]
+
+    def run(order):
+        sends = []
+        for h in order:
+            halo[h].wait_recv()
+            prepped = prep(h)
             for k in range(depth):
-                copy(g, k, p, nhalo).wait_recv()
-                add(g, k)
-    for c in sends:
-        c.wait_send()
-    out_ref[...] = out_ref[...] * factor
-
+                halo[2 + 2 * k + h].wait_recv()
+                smooth(k, h, prepped)
+                for i, p in enumerate([zp] + peers):
+                    c = copy(me, k, h, p, i)
+                    c.start()
+                    sends.append(c)
+        for c in halo:
+            c.wait_send()
+        out_ref[...] = jnp.zeros(out_ref.shape, out_ref.dtype)
+        loads[4].wait()
+        for k in range(depth):
+            add(me, k)
+        for h in order:
+            for k in range(depth):
+                copy(zp, k, h, zp, 0).wait_recv()
+                for i, p in enumerate(peers):
+                    c = copy(zp, k, h, p, half + i)
+                    c.start()
+                    sends.append(c)
+        for k in range(depth):
+            add(zp, k)
+        for p in peers:
+            for g in (p, lax.rem(p + half, groups)):
+                for h in order:
+                    for k in range(depth):
+                        copy(g, k, h, p, 0).wait_recv()
+                for k in range(depth):
+                    add(g, k)
+        for c in sends:
+            c.wait_send()
+        out_ref[...] = out_ref[...] * factor
+
+    core = lax.rem(tile, 2)
+
+    @pl.when(core == 0)
+    def _():
+        run((1, 0))
+
+    @pl.when(core == 1)
+    def _():
+        run((0, 1))
 
 def on_device(controls, perturbations, owner, land_mask, diffusivity):
     groups = lax.axis_size("tm")
@@ -175,8 +195,8 @@
             pltpu.VMEM((rows + 2 * width, ny), land_mask.dtype),
             pltpu.VMEM((groups * depth, rows, lev, ny), jnp.bfloat16),
             pltpu.VMEM(pert.shape, pert.dtype),
-            pltpu.SemaphoreType.DMA((2 + 2 * depth + 2 * half * depth,)),
-            pltpu.SemaphoreType.DMA((2 + 2 * depth + groups * depth,)),
+            pltpu.SemaphoreType.DMA((2 + 2 * depth + 2 * depth * (2 * half - 1),)),
+            pltpu.SemaphoreType.DMA((2 + 2 * depth + 2 * groups * depth,)),
             pltpu.SemaphoreType.DMA((5,)),
         ],
         compiler_params=pltpu.CompilerParams(

time: 43.7 us -> 44.9 us (1.027)
  the two profiles are of different devices: /device:TPU:38 before, /device:TPU:1 now
where the time goes in v10:
time: 44.9 us; the launch traced here: 44.7 us
  Pallas kernels  42.9 us (96%)
  local copies, waits for them, and re-layouts  1.87 us (4%)
    pallas_call x1, Pallas kernels, on_device(): pl.pallas_call(functools.partial(fused_kernel, half, width, factor), out_...  42.9 us
    unnamed x1, local copies, waits for them, and re-layouts  1.87 us

profile of v10, /device:TPU:1, one launch (start us, length us, event | category | flops | bytes accessed | tf_op | source)
XLA Modules:
  0.0 44.7 jit_solution(7146420793372792791)
XLA Ops:
  0.0 42.9 %shard_map.55 = f32[4,8,8,512]{3,2,1,0:T(8,128)} custom-call(s32[16]{0:T(128)} %owner_hbm.1, f32[2,8]{1,0:T(2,128)} %diff_hbm.1, f32[2,8,8,512]{3,2,1,0:T(8,128)} %ctrl_hbm.1, s32[8,512]{1,0:T(8,128)} %mask_hbm.1, bf16[16,4,8,8,512]{4,3,2,1,0:T(8,128)(2,1)} %bitcast.2), custom_call_target="tpu_custom_call" | custom-call | tf_op jit(solution)/shard_map/pallas_call | solution.py:184
  42.9 1.9 %copy.7 = f32[1,4,8,8,512]{4,3,2,1,0:T(8,128)} copy(f32[1,4,8,8,512]{4,3,2,1,0:T(8,128)} %bitcast.3) | data formatting | bytes 1048576

commit v11 on v9

--- a/solution.py
+++ b/solution.py
@@ -26,7 +26,7 @@
 
 
 def fused_kernel(half, width, factor, owner_hbm, diff_hbm, ctrl_hbm, mask_hbm, pert_hbm,
-                 out_ref, owner_ref, diff_ref, ctrl_ref, mask_ref, ext, mext, held, pert,
+                 out_ref, owner_ref, diff_ref, ext, mext, held, pert,
                  send_sem, recv_sem, load_sem):
     tile = lax.axis_index("tile")
     count = lax.axis_size("tile")
@@ -41,32 +41,30 @@
     base = me - lax.rem(me, half)
     peers = [base + lax.rem(lax.rem(me, half) + d, half) for d in range(1, half)]
 
+    barrier = pltpu.get_barrier_semaphore()
+    for dev in ((left, me), (right, me), (tile, zp)) + tuple((tile, p) for p in peers):
+        pl.semaphore_signal(barrier, inc=1, device_id=dev, device_id_type=MESH)
+
     loads = [
         pltpu.make_async_copy(src, dst, load_sem.at[i])
         for i, (src, dst) in enumerate(
-            [(ctrl_hbm, ctrl_ref), (mask_hbm, mask_ref), (diff_hbm, diff_ref),
-             (owner_hbm, owner_ref), (pert_hbm, pert)]
+            [(ctrl_hbm, ext.at[:, pl.ds(width, rows)]), (mask_hbm, mext.at[pl.ds(width, rows)]),
+             (diff_hbm, diff_ref), (owner_hbm, owner_ref), (pert_hbm, pert)]
         )
     ]
     for c in loads:
         c.start()
-    for c in loads[:4]:
-        c.wait()
-
-    barrier = pltpu.get_barrier_semaphore()
-    for dev in ((left, me), (right, me), (tile, zp)) + tuple((tile, p) for p in peers):
-        pl.semaphore_signal(barrier, inc=1, device_id=dev, device_id_type=MESH)
     pl.semaphore_wait(barrier, 2 + half)
 
     head, tail = pl.ds(0, width), pl.ds(rows - width, width)
     before, after = pl.ds(0, width), pl.ds(width + rows, width)
     plan = [
-        (mask_ref.at[tail], mext.at[before], right),
-        (mask_ref.at[head], mext.at[after], left),
+        (mask_hbm.at[tail], mext.at[before], right),
+        (mask_hbm.at[head], mext.at[after], left),
     ]
     for k in range(depth):
-        plan.append((ctrl_ref.at[k, tail], ext.at[k, before], right))
-        plan.append((ctrl_ref.at[k, head], ext.at[k, after], left))
+        plan.append((ctrl_hbm.at[k, tail], ext.at[k, before], right))
+        plan.append((ctrl_hbm.at[k, head], ext.at[k, after], left))
     halo = []
     for i, (src, dst, dev) in enumerate(plan):
         c = pltpu.make_async_remote_copy(
@@ -75,8 +73,8 @@
         )
         c.start()
         halo.append(c)
-    ext[:, pl.ds(width, rows)] = ctrl_ref[...]
-    mext[pl.ds(width, rows)] = mask_ref[...]
+    for c in loads[:4]:
+        c.wait()
     for c in halo[:2]:
         c.wait_recv()
 
@@ -169,8 +167,6 @@
         scratch_shapes=[
             pltpu.SMEM(owner.shape, owner.dtype),
             pltpu.SMEM(diffusivity.shape, diffusivity.dtype),
-            pltpu.VMEM(controls.shape, controls.dtype),
-            pltpu.VMEM(land_mask.shape, land_mask.dtype),
             pltpu.VMEM((depth, rows + 2 * width, lev, ny), controls.dtype),
             pltpu.VMEM((rows + 2 * width, ny), land_mask.dtype),
             pltpu.VMEM((groups * depth, rows, lev, ny), jnp.bfloat16),

time: 43.7 us -> 43 us (0.984)
  Pallas kernels: 41.7 us -> 41 us
    pallas_call x1, Pallas kernels: 41.7 us -> 41 us  [on_device(): pl.pallas_call(functools.partial(fused_kernel, half, width, factor), out_...]
where the time goes in v11:
time: 43 us; the launch traced here: 42.9 us
  Pallas kernels  41 us (95%)
  local copies, waits for them, and re-layouts  1.87 us (4%)
    pallas_call x1, Pallas kernels, on_device(): pl.pallas_call(functools.partial(fused_kernel, half, width, factor), out_...  41 us
    unnamed x1, local copies, waits for them, and re-layouts  1.87 us

profile of v11, /device:TPU:38, one launch (start us, length us, event | category | flops | bytes accessed | tf_op | source)
XLA Modules:
  0.0 42.9 jit_solution(8870786968945363455)
XLA Ops:
  0.0 41.0 %shard_map.55 = f32[4,8,8,512]{3,2,1,0:T(8,128)} custom-call(s32[16]{0:T(128)} %owner_hbm.1, f32[2,8]{1,0:T(2,128)} %diff_hbm.1, f32[2,8,8,512]{3,2,1,0:T(8,128)} %ctrl_hbm.1, s32[8,512]{1,0:T(8,128)} %mask_hbm.1, bf16[16,4,8,8,512]{4,3,2,1,0:T(8,128)(2,1)} %bitcast.2), custom_call_target="tpu_custom_call" | custom-call | tf_op jit(solution)/shard_map/pallas_call | solution.py:162
  41.0 1.9 %copy.7 = f32[1,4,8,8,512]{4,3,2,1,0:T(8,128)} copy(f32[1,4,8,8,512]{4,3,2,1,0:T(8,128)} %bitcast.3) | data formatting | bytes 1048576

commit v12 on v11

--- a/solution.py
+++ b/solution.py
@@ -103,9 +103,10 @@
             recv_sem=recv_sem.at[nhalo + g * depth + k], device_id=(tile, dev), device_id_type=MESH,
         )
 
-    def add(g, k):
+    def add(g, k, scale=None):
         member = owner_ref[g * depth + k]
-        out_ref[...] += pert[member].astype(jnp.float32) * held[g * depth + k].astype(jnp.float32)[None]
+        total = out_ref[...] + pert[member].astype(jnp.float32) * held[g * depth + k].astype(jnp.float32)[None]
+        out_ref[...] = total if scale is None else total * scale
 
     sends = []
     for k in range(depth):
@@ -141,13 +142,17 @@
             sends.append(c)
         add(zp, k)
     for p in peers:
-        for g in (p, lax.rem(p + half, groups)):
-            for k in range(depth):
-                copy(g, k, p, nhalo).wait_recv()
-                add(g, k)
+        for k in range(depth):
+            copy(p, k, p, nhalo).wait_recv()
+            add(p, k)
+    for j, p in enumerate(peers):
+        far = lax.rem(p + half, groups)
+        for k in range(depth):
+            copy(far, k, p, nhalo).wait_recv()
+            last = j == len(peers) - 1 and k == depth - 1
+            add(far, k, factor if last else None)
     for c in sends:
         c.wait_send()
-    out_ref[...] = out_ref[...] * factor
 
 
 def on_device(controls, perturbations, owner, land_mask, diffusivity):

time: 43 us -> 42.9 us (level)
  no operation moved by 1% of the time
where the time goes in v12:
time: 42.9 us; the launch traced here: 42.7 us
  Pallas kernels  40.8 us (95%)
  local copies, waits for them, and re-layouts  1.87 us (4%)
    pallas_call x1, Pallas kernels, on_device(): pl.pallas_call(functools.partial(fused_kernel, half, width, factor), out_...  40.8 us
    unnamed x1, local copies, waits for them, and re-layouts  1.87 us

profile of v12, /device:TPU:38, one launch (start us, length us, event | category | flops | bytes accessed | tf_op | source)
XLA Modules:
  0.0 42.7 jit_solution(7209049692565176600)
XLA Ops:
  0.0 40.8 %shard_map.55 = f32[4,8,8,512]{3,2,1,0:T(8,128)} custom-call(s32[16]{0:T(128)} %owner_hbm.1, f32[2,8]{1,0:T(2,128)} %diff_hbm.1, f32[2,8,8,512]{3,2,1,0:T(8,128)} %ctrl_hbm.1, s32[8,512]{1,0:T(8,128)} %mask_hbm.1, bf16[16,4,8,8,512]{4,3,2,1,0:T(8,128)(2,1)} %bitcast.2), custom_call_target="tpu_custom_call" | custom-call | tf_op jit(solution)/shard_map/pallas_call | solution.py:167
  40.8 1.9 %copy.7 = f32[1,4,8,8,512]{4,3,2,1,0:T(8,128)} copy(f32[1,4,8,8,512]{4,3,2,1,0:T(8,128)} %bitcast.3) | data formatting | bytes 1048576

commit v13 on v12

--- a/solution.py
+++ b/solution.py
@@ -26,7 +26,7 @@
 
 
 def fused_kernel(half, width, factor, owner_hbm, diff_hbm, ctrl_hbm, mask_hbm, pert_hbm,
-                 out_ref, owner_ref, diff_ref, ext, mext, held, pert,
+                 out_hbm, owner_ref, diff_ref, ext, mext, held, pert, out_ref,
                  send_sem, recv_sem, load_sem):
     tile = lax.axis_index("tile")
     count = lax.axis_size("tile")
@@ -151,8 +151,11 @@
             copy(far, k, p, nhalo).wait_recv()
             last = j == len(peers) - 1 and k == depth - 1
             add(far, k, factor if last else None)
+    store = pltpu.make_async_copy(out_ref, out_hbm, load_sem.at[5])
+    store.start()
     for c in sends:
         c.wait_send()
+    store.wait()
 
 
 def on_device(controls, perturbations, owner, land_mask, diffusivity):
@@ -168,7 +171,7 @@
         functools.partial(fused_kernel, half, width, factor),
         out_shape=jax.ShapeDtypeStruct(pert.shape[1:], jnp.float32),
         in_specs=[hbm] * 5,
-        out_specs=vmem,
+        out_specs=hbm,
         scratch_shapes=[
             pltpu.SMEM(owner.shape, owner.dtype),
             pltpu.SMEM(diffusivity.shape, diffusivity.dtype),
@@ -176,9 +179,10 @@
             pltpu.VMEM((rows + 2 * width, ny), land_mask.dtype),
             pltpu.VMEM((groups * depth, rows, lev, ny), jnp.bfloat16),
             pltpu.VMEM(pert.shape, pert.dtype),
+            pltpu.VMEM(pert.shape[1:], jnp.float32),
             pltpu.SemaphoreType.DMA((2 + 2 * depth + 2 * half * depth,)),
             pltpu.SemaphoreType.DMA((2 + 2 * depth + groups * depth,)),
-            pltpu.SemaphoreType.DMA((5,)),
+            pltpu.SemaphoreType.DMA((6,)),
         ],
         compiler_params=pltpu.CompilerParams(
             collective_id=0, has_side_effects=True, vmem_limit_bytes=64 * 1024 * 1024

time: 42.9 us -> 42.8 us (level)
  no operation moved by 1% of the time
where the time goes in v13:
time: 42.8 us; the launch traced here: 42.7 us
  Pallas kernels  40.8 us (95%)
  local copies, waits for them, and re-layouts  1.87 us (4%)
    pallas_call x1, Pallas kernels, on_device(): pl.pallas_call(functools.partial(fused_kernel, half, width, factor), out_...  40.8 us
    unnamed x1, local copies, waits for them, and re-layouts  1.87 us

profile of v13, /device:TPU:38, one launch (start us, length us, event | category | flops | bytes accessed | tf_op | source)
XLA Modules:
  0.0 42.7 jit_solution(16958349667656065848)
XLA Ops:
  0.0 40.8 %shard_map.55 = f32[4,8,8,512]{3,2,1,0:T(8,128)} custom-call(s32[16]{0:T(128)} %owner_hbm.1, f32[2,8]{1,0:T(2,128)} %diff_hbm.1, f32[2,8,8,512]{3,2,1,0:T(8,128)} %ctrl_hbm.1, s32[8,512]{1,0:T(8,128)} %mask_hbm.1, bf16[16,4,8,8,512]{4,3,2,1,0:T(8,128)(2,1)} %bitcast.2), custom_call_target="tpu_custom_call" | custom-call | tf_op jit(solution)/shard_map/pallas_call | solution.py:170
  40.8 1.9 %copy.7 = f32[1,4,8,8,512]{4,3,2,1,0:T(8,128)} copy(f32[1,4,8,8,512]{4,3,2,1,0:T(8,128)} %bitcast.3) | data formatting | bytes 1048576

commit v14 on v12

--- a/solution.py
+++ b/solution.py
@@ -123,8 +123,12 @@
             flux = flux + ayp[lo:hi] * (uyp - centre)
             u = jnp.where(kept[lo:hi], centre + flux, 0.0)
         held[me * depth + k] = u.astype(held.dtype)
-        for i, p in enumerate([zp] + peers):
-            c = copy(me, k, p, nhalo + k * 2 * half + i)
+        c = copy(me, k, zp, nhalo + k * 2 * half)
+        c.start()
+        sends.append(c)
+    for k in range(depth):
+        for i, p in enumerate(peers):
+            c = copy(me, k, p, nhalo + k * 2 * half + 1 + i)
             c.start()
             sends.append(c)
 

time: 42.9 us -> 42.9 us (level)
  no operation moved by 1% of the time
where the time goes in v14:
time: 42.9 us; the launch traced here: 42.7 us
  Pallas kernels  40.8 us (95%)
  local copies, waits for them, and re-layouts  1.87 us (4%)
    pallas_call x1, Pallas kernels, on_device(): pl.pallas_call(functools.partial(fused_kernel, half, width, factor), out_...  40.8 us
    unnamed x1, local copies, waits for them, and re-layouts  1.87 us

profile of v14, /device:TPU:38, one launch (start us, length us, event | category | flops | bytes accessed | tf_op | source)
XLA Modules:
  0.0 42.7 jit_solution(16902722917013365616)
XLA Ops:
  0.0 40.8 %shard_map.55 = f32[4,8,8,512]{3,2,1,0:T(8,128)} custom-call(s32[16]{0:T(128)} %owner_hbm.1, f32[2,8]{1,0:T(2,128)} %diff_hbm.1, f32[2,8,8,512]{3,2,1,0:T(8,128)} %ctrl_hbm.1, s32[8,512]{1,0:T(8,128)} %mask_hbm.1, bf16[16,4,8,8,512]{4,3,2,1,0:T(8,128)(2,1)} %bitcast.2), custom_call_target="tpu_custom_call" | custom-call | tf_op jit(solution)/shard_map/pallas_call | solution.py:171
  40.8 1.9 %copy.7 = f32[1,4,8,8,512]{4,3,2,1,0:T(8,128)} copy(f32[1,4,8,8,512]{4,3,2,1,0:T(8,128)} %bitcast.3) | data formatting | bytes 1048576

commit v15 on v12

--- a/solution.py
+++ b/solution.py
@@ -52,7 +52,7 @@
              (diff_hbm, diff_ref), (owner_hbm, owner_ref), (pert_hbm, pert)]
         )
     ]
-    for c in loads:
+    for c in loads[:4]:
         c.start()
     pl.semaphore_wait(barrier, 2 + half)
 
@@ -73,6 +73,7 @@
         )
         c.start()
         halo.append(c)
+    loads[4].start()
     for c in loads[:4]:
         c.wait()
     for c in halo[:2]:

time: 42.9 us -> 42.9 us (level)
  no operation moved by 1% of the time
where the time goes in v15:
time: 42.9 us; the launch traced here: 42.7 us
  Pallas kernels  40.8 us (95%)
  local copies, waits for them, and re-layouts  1.87 us (4%)
    pallas_call x1, Pallas kernels, on_device(): pl.pallas_call(functools.partial(fused_kernel, half, width, factor), out_...  40.8 us
    unnamed x1, local copies, waits for them, and re-layouts  1.87 us

profile of v15, /device:TPU:38, one launch (start us, length us, event | category | flops | bytes accessed | tf_op | source)
XLA Modules:
  0.0 42.7 jit_solution(12854320793107667374)
XLA Ops:
  0.0 40.8 %shard_map.55 = f32[4,8,8,512]{3,2,1,0:T(8,128)} custom-call(s32[16]{0:T(128)} %owner_hbm.1, f32[2,8]{1,0:T(2,128)} %diff_hbm.1, f32[2,8,8,512]{3,2,1,0:T(8,128)} %ctrl_hbm.1, s32[8,512]{1,0:T(8,128)} %mask_hbm.1, bf16[16,4,8,8,512]{4,3,2,1,0:T(8,128)(2,1)} %bitcast.2), custom_call_target="tpu_custom_call" | custom-call | tf_op jit(solution)/shard_map/pallas_call | solution.py:168
  40.8 1.9 %copy.7 = f32[1,4,8,8,512]{4,3,2,1,0:T(8,128)} copy(f32[1,4,8,8,512]{4,3,2,1,0:T(8,128)} %bitcast.3) | data formatting | bytes 1048576

commit v16 on v12

--- a/solution.py
+++ b/solution.py
@@ -75,9 +75,6 @@
         halo.append(c)
     for c in loads[:4]:
         c.wait()
-    for c in halo[:2]:
-        c.wait_recv()
-
     grow = tile * rows - width + lax.broadcasted_iota(jnp.int32, (wide, lev, ny), 0)
     inside = (grow >= 0) & (grow < count * rows)
     levels = lax.broadcasted_iota(jnp.int32, (wide, lev, ny), 1)
@@ -86,6 +83,8 @@
     for l in range(lev):
         sea = jnp.where(levels == l, diff_ref[0, l], sea)
         land = jnp.where(levels == l, diff_ref[1, l], land)
+    for c in halo[:2]:
+        c.wait_recv()
     landed = jnp.broadcast_to(mext[...][:, None, :], (wide, lev, ny)) == 1
     coef = jnp.where(inside, jnp.where(landed, land, sea), 0.0)
     mid = coef[1:-1]

time: 42.9 us -> 42.9 us (level)
  no operation moved by 1% of the time
where the time goes in v16:
time: 42.9 us; the launch traced here: 42.7 us
  Pallas kernels  40.8 us (95%)
  local copies, waits for them, and re-layouts  1.87 us (4%)
    pallas_call x1, Pallas kernels, on_device(): pl.pallas_call(functools.partial(fused_kernel, half, width, factor), out_...  40.8 us
    unnamed x1, local copies, waits for them, and re-layouts  1.87 us

profile of v16, /device:TPU:38, one launch (start us, length us, event | category | flops | bytes accessed | tf_op | source)
XLA Modules:
  0.0 42.7 jit_solution(17080598539962946890)
XLA Ops:
  0.0 40.8 %shard_map.55 = f32[4,8,8,512]{3,2,1,0:T(8,128)} custom-call(s32[16]{0:T(128)} %owner_hbm.1, f32[2,8]{1,0:T(2,128)} %diff_hbm.1, f32[2,8,8,512]{3,2,1,0:T(8,128)} %ctrl_hbm.1, s32[8,512]{1,0:T(8,128)} %mask_hbm.1, bf16[16,4,8,8,512]{4,3,2,1,0:T(8,128)(2,1)} %bitcast.2), custom_call_target="tpu_custom_call" | custom-call | tf_op jit(solution)/shard_map/pallas_call | solution.py:166
  40.8 1.9 %copy.7 = f32[1,4,8,8,512]{4,3,2,1,0:T(8,128)} copy(f32[1,4,8,8,512]{4,3,2,1,0:T(8,128)} %bitcast.3) | data formatting | bytes 1048576

commit v17 on v16

--- a/solution.py
+++ b/solution.py
@@ -13,12 +13,17 @@
 SWEEPS = 4
 
 
-def lane_shifts(u):
+def lane_masks(shape):
+    ny = shape[-1]
+    lane = lax.broadcasted_iota(jnp.int32, shape, len(shape) - 1)
+    rolled = pltpu.roll(lane, 1, len(shape) - 1)
+    return lane, (rolled == lane - 1) | (rolled == lane + ny - 1)
+
+
+def lane_shifts(u, masks):
     ny = u.shape[-1]
-    lane = lax.broadcasted_iota(jnp.int32, u.shape, u.ndim - 1)
+    lane, moved = masks[0][:u.shape[0]], masks[1][:u.shape[0]]
     fwd, back = pltpu.roll(u, 1, u.ndim - 1), pltpu.roll(u, ny - 1, u.ndim - 1)
-    rolled = pltpu.roll(lane, 1, u.ndim - 1)
-    moved = (rolled == lane - 1) | (rolled == lane + ny - 1)
     lower = jnp.where(moved, fwd, back)
     upper = jnp.where(moved, back, fwd)
     zero = jnp.zeros_like(u)
@@ -88,7 +93,8 @@
     landed = jnp.broadcast_to(mext[...][:, None, :], (wide, lev, ny)) == 1
     coef = jnp.where(inside, jnp.where(landed, land, sea), 0.0)
     mid = coef[1:-1]
-    cym, cyp = lane_shifts(mid)
+    masks = lane_masks(mid.shape)
+    cym, cyp = lane_shifts(mid, masks)
     axm, axp = 0.5 * (mid + coef[:-2]), 0.5 * (mid + coef[2:])
     aym, ayp = 0.5 * (mid + cym), 0.5 * (mid + cyp)
     kept = inside[1:-1]
@@ -115,7 +121,7 @@
         for sweep_index in range(SWEEPS):
             lo, hi = sweep_index, wide - 2 - sweep_index
             centre = u[1:-1]
-            uym, uyp = lane_shifts(centre)
+            uym, uyp = lane_shifts(centre, masks)
             flux = axm[lo:hi] * (u[:-2] - centre)
             flux = flux + axp[lo:hi] * (u[2:] - centre)
             flux = flux + aym[lo:hi] * (uym - centre)

time: 42.9 us -> 42.9 us (level)
  no operation moved by 1% of the time
where the time goes in v17:
time: 42.9 us; the launch traced here: 42.7 us
  Pallas kernels  40.8 us (95%)
  local copies, waits for them, and re-layouts  1.87 us (4%)
    pallas_call x1, Pallas kernels, on_device(): pl.pallas_call(functools.partial(fused_kernel, half, width, factor), out_...  40.8 us
    unnamed x1, local copies, waits for them, and re-layouts  1.87 us

profile of v17, /device:TPU:38, one launch (start us, length us, event | category | flops | bytes accessed | tf_op | source)
XLA Modules:
  0.0 42.7 jit_solution(11730868893595547678)
XLA Ops:
  0.0 40.8 %shard_map.55 = f32[4,8,8,512]{3,2,1,0:T(8,128)} custom-call(s32[16]{0:T(128)} %owner_hbm.1, f32[2,8]{1,0:T(2,128)} %diff_hbm.1, f32[2,8,8,512]{3,2,1,0:T(8,128)} %ctrl_hbm.1, s32[8,512]{1,0:T(8,128)} %mask_hbm.1, bf16[16,4,8,8,512]{4,3,2,1,0:T(8,128)(2,1)} %bitcast.2), custom_call_target="tpu_custom_call" | custom-call | tf_op jit(solution)/shard_map/pallas_call | solution.py:172
  40.8 1.9 %copy.7 = f32[1,4,8,8,512]{4,3,2,1,0:T(8,128)} copy(f32[1,4,8,8,512]{4,3,2,1,0:T(8,128)} %bitcast.3) | data formatting | bytes 1048576

commit v18 on v16

--- a/solution.py
+++ b/solution.py
@@ -102,9 +102,10 @@
             recv_sem=recv_sem.at[nhalo + g * depth + k], device_id=(tile, dev), device_id_type=MESH,
         )
 
-    def add(g, k, scale=None):
+    def add(g, k, scale=None, first=False):
         member = owner_ref[g * depth + k]
-        total = out_ref[...] + pert[member].astype(jnp.float32) * held[g * depth + k].astype(jnp.float32)[None]
+        term = pert[member].astype(jnp.float32) * held[g * depth + k].astype(jnp.float32)[None]
+        total = term if first else out_ref[...] + term
         out_ref[...] = total if scale is None else total * scale
 
     sends = []
@@ -129,10 +130,9 @@
 
     for c in halo:
         c.wait_send()
-    out_ref[...] = jnp.zeros(out_ref.shape, out_ref.dtype)
     loads[4].wait()
     for k in range(depth):
-        add(me, k)
+        add(me, k, first=k == 0)
     for k in range(depth):
         copy(zp, k, zp, nhalo).wait_recv()
         for i, p in enumerate(peers):

time: 42.9 us -> 42.9 us (level)
  no operation moved by 1% of the time
where the time goes in v18:
time: 42.9 us; the launch traced here: 42.7 us
  Pallas kernels  40.8 us (95%)
  local copies, waits for them, and re-layouts  1.87 us (4%)
    pallas_call x1, Pallas kernels, on_device(): pl.pallas_call(functools.partial(fused_kernel, half, width, factor), out_...  40.8 us
    unnamed x1, local copies, waits for them, and re-layouts  1.87 us

profile of v18, /device:TPU:38, one launch (start us, length us, event | category | flops | bytes accessed | tf_op | source)
XLA Modules:
  0.0 42.7 jit_solution(16379858441825970880)
XLA Ops:
  0.0 40.8 %shard_map.55 = f32[4,8,8,512]{3,2,1,0:T(8,128)} custom-call(s32[16]{0:T(128)} %owner_hbm.1, f32[2,8]{1,0:T(2,128)} %diff_hbm.1, f32[2,8,8,512]{3,2,1,0:T(8,128)} %ctrl_hbm.1, s32[8,512]{1,0:T(8,128)} %mask_hbm.1, bf16[16,4,8,8,512]{4,3,2,1,0:T(8,128)(2,1)} %bitcast.2), custom_call_target="tpu_custom_call" | custom-call | tf_op jit(solution)/shard_map/pallas_call | solution.py:166
  40.8 1.9 %copy.7 = f32[1,4,8,8,512]{4,3,2,1,0:T(8,128)} copy(f32[1,4,8,8,512]{4,3,2,1,0:T(8,128)} %bitcast.3) | data formatting | bytes 1048576

commit v19 on v16

--- a/solution.py
+++ b/solution.py
@@ -139,6 +139,7 @@
             c = copy(zp, k, p, nhalo + k * 2 * half + half + i)
             c.start()
             sends.append(c)
+    for k in range(depth):
         add(zp, k)
     for p in peers:
         for k in range(depth):

time: 42.9 us -> 42.9 us (level)
  no operation moved by 1% of the time
where the time goes in v19:
time: 42.9 us; the launch traced here: 42.7 us
  Pallas kernels  40.8 us (95%)
  local copies, waits for them, and re-layouts  1.87 us (4%)
    pallas_call x1, Pallas kernels, on_device(): pl.pallas_call(functools.partial(fused_kernel, half, width, factor), out_...  40.8 us
    unnamed x1, local copies, waits for them, and re-layouts  1.87 us

profile of v19, /device:TPU:38, one launch (start us, length us, event | category | flops | bytes accessed | tf_op | source)
XLA Modules:
  0.0 42.7 jit_solution(8128304997105085535)
XLA Ops:
  0.0 40.8 %shard_map.55 = f32[4,8,8,512]{3,2,1,0:T(8,128)} custom-call(s32[16]{0:T(128)} %owner_hbm.1, f32[2,8]{1,0:T(2,128)} %diff_hbm.1, f32[2,8,8,512]{3,2,1,0:T(8,128)} %ctrl_hbm.1, s32[8,512]{1,0:T(8,128)} %mask_hbm.1, bf16[16,4,8,8,512]{4,3,2,1,0:T(8,128)(2,1)} %bitcast.2), custom_call_target="tpu_custom_call" | custom-call | tf_op jit(solution)/shard_map/pallas_call | solution.py:167
  40.8 1.9 %copy.7 = f32[1,4,8,8,512]{4,3,2,1,0:T(8,128)} copy(f32[1,4,8,8,512]{4,3,2,1,0:T(8,128)} %bitcast.3) | data formatting | bytes 1048576

commit v20 on v16

--- a/solution.py
+++ b/solution.py
@@ -42,7 +42,7 @@
     peers = [base + lax.rem(lax.rem(me, half) + d, half) for d in range(1, half)]
 
     barrier = pltpu.get_barrier_semaphore()
-    for dev in ((left, me), (right, me), (tile, zp)) + tuple((tile, p) for p in peers):
+    for dev in ((tile, zp), (left, me), (right, me)) + tuple((tile, p) for p in peers):
         pl.semaphore_signal(barrier, inc=1, device_id=dev, device_id_type=MESH)
 
     loads = [

time: 42.9 us -> 42.8 us (level)
  no operation moved by 1% of the time
where the time goes in v20:
time: 42.8 us; the launch traced here: 42.7 us
  Pallas kernels  40.8 us (95%)
  local copies, waits for them, and re-layouts  1.87 us (4%)
    pallas_call x1, Pallas kernels, on_device(): pl.pallas_call(functools.partial(fused_kernel, half, width, factor), out_...  40.8 us
    unnamed x1, local copies, waits for them, and re-layouts  1.87 us

profile of v20, /device:TPU:38, one launch (start us, length us, event | category | flops | bytes accessed | tf_op | source)
XLA Modules:
  0.0 42.7 jit_solution(7588282498318644259)
XLA Ops:
  0.0 40.8 %shard_map.55 = f32[4,8,8,512]{3,2,1,0:T(8,128)} custom-call(s32[16]{0:T(128)} %owner_hbm.1, f32[2,8]{1,0:T(2,128)} %diff_hbm.1, f32[2,8,8,512]{3,2,1,0:T(8,128)} %ctrl_hbm.1, s32[8,512]{1,0:T(8,128)} %mask_hbm.1, bf16[16,4,8,8,512]{4,3,2,1,0:T(8,128)(2,1)} %bitcast.2), custom_call_target="tpu_custom_call" | custom-call | tf_op jit(solution)/shard_map/pallas_call | solution.py:166
  40.8 1.9 %copy.7 = f32[1,4,8,8,512]{4,3,2,1,0:T(8,128)} copy(f32[1,4,8,8,512]{4,3,2,1,0:T(8,128)} %bitcast.3) | data formatting | bytes 1048576
